TPU v7x, 128 devices: a whole 4x4x4 slice. The times are simulated.
128 devices in a mesh: section: 8 (over y, core), expert: 16 (over x, z).
Axes of the slice: x: 4, y: 4, z: 4, core: 2. Of those that a mesh axis runs over, the one named last changes fastest.
Arguments:
- section_input: bfloat16 [8, 2048, 2880], P('section', 'expert'), may hold values from -6 to 6
- attention_gain: float32 [8, 2880], P('section'), may hold values from 0.1 to 1.9
- query_key_value_weight: bfloat16 [8, 2880, 2560], P('section', 'expert'), may hold values from -0.109375 to 0.109375
- qkv_bias: float32 [8, 2560], P('section'), may hold values from -3 to 8
- out_weight: bfloat16 [8, 2048, 2880], P('section'), may hold values from -0.125 to 0.125
- out_bias: float32 [8, 2880], P('section'), may hold values from -3 to 3
- attention_sink_logits: float32 [8, 32], P('section'), may hold values from -1 to 250
- expert_gain: float32 [8, 2880], P('section'), may hold values from 0.1 to 1.9
- gate_up_weight: bfloat16 [8, 16, 2880, 1440], P('section', 'expert'), may hold values from -0.109375 to 0.109375
- down_weight: bfloat16 [8, 16, 720, 2880], P('section', 'expert'), may hold values from -0.15625 to 0.15625
- expert_ids: int32 [8, 2048, 4], P('section', 'expert'), may hold values from 0 to 7, all different within a row; in each aligned block of 128 rows (0 to 127, 128 to 255, ..., all dimensions but the last counted through in order) at most 80 rows name the same one
- gate_logits: float32 [8, 2048, 4], P('section', 'expert'), may hold values from -8 to 204
- placement: int32 [8, 8], P('section'), may hold values from 0 to 7, each once within a row
Outputs:
- section_output: bfloat16 [8, 2048, 2880], P('section', 'expert')
Inputs may be any that keep to these rules, and one draw needn't show every extreme that they name: `expert_ids`: within each section, among the 128 tokens of one device no expert is named more than 80 times, a bound that some block reaches. `placement`: each row names every expert once.
All inputs are finite; a program needn't handle non-finite values.
Results may differ from a plain program's by a relative error of at most 0.018.
Values may be sent and summed in bfloat16 or wider, within the bound.
A program may use at most 128 MiB of HBM per device.

v0:
```python
import jax
import jax.numpy as jnp
from jax import lax
from jax.sharding import PartitionSpec as P

HEAD_DIM = 64
QUERY_HEADS = 32
KEY_VALUE_HEADS = 4
WINDOW_TOKENS = 128
TOP = 4


def from_behind(x, axis, by):
    size = lax.axis_size(axis)
    pairs = [(i, i + by) for i in range(size) if 0 <= i + by < size]
    return lax.ppermute(x, axis, pairs)


def passed_along(x, axis, by):
    size = lax.axis_size(axis)
    return lax.ppermute(x, axis, [(i, (i + by) % size) for i in range(size)])


def normed(vector, gain_row):
    as_float = vector.astype(jnp.float32)
    inverse_rms = lax.rsqrt(jnp.mean(as_float * as_float, axis=-1, keepdims=True) + 1e-05)
    return (as_float * inverse_rms * gain_row).astype(jnp.bfloat16)


def swiglu(hidden):
    half_cols = hidden.shape[1] // 2
    gate_part = hidden[:, :half_cols]
    up_part = hidden[:, half_cols:]
    return ((up_part + 1.0) * gate_part * jax.nn.sigmoid(1.702 * gate_part)).astype(jnp.bfloat16)


def shards(
    section_input,
    attention_gain,
    query_key_value_weight,
    qkv_bias,
    out_weight,
    out_bias,
    attention_sink_logits,
    expert_gain,
    gate_up_weight,
    down_weight,
    expert_ids,
    gate_logits,
    placement,
):
    count_of_rows = section_input.shape[1]
    model_width = section_input.shape[2]
    experts_count = placement.shape[1]
    slot_count = 2 * min(count_of_rows // 2, count_of_rows * TOP * 5 // (8 * experts_count))
    offset = lax.axis_index("expert") * count_of_rows
    query_group_width = QUERY_HEADS // KEY_VALUE_HEADS
    tile_gu = gate_up_weight[0, 0]
    tile_down = down_weight[0, 0]
    state = section_input[0]
    normed_in = normed(state, attention_gain[0])
    projected_rows = (
        jnp.dot(
            normed_in,
            lax.all_gather(query_key_value_weight[0], "expert", axis=0, tiled=True),
            preferred_element_type=jnp.float32,
        )
        + qkv_bias[0]
    ).astype(jnp.bfloat16)
    query_rows = projected_rows[:, : QUERY_HEADS * HEAD_DIM].reshape(
        count_of_rows, KEY_VALUE_HEADS, query_group_width, HEAD_DIM
    )
    key_value = projected_rows[:, QUERY_HEADS * HEAD_DIM :]
    rim_rows = from_behind(key_value, "expert", 1)
    rows_in_window = jnp.concatenate([rim_rows, key_value], 0)
    key_row_slice = rows_in_window[:, : KEY_VALUE_HEADS * HEAD_DIM].reshape(
        WINDOW_TOKENS + count_of_rows, KEY_VALUE_HEADS, HEAD_DIM
    )
    value_row_slice = rows_in_window[:, KEY_VALUE_HEADS * HEAD_DIM :].reshape(
        WINDOW_TOKENS + count_of_rows, KEY_VALUE_HEADS, HEAD_DIM
    )
    scores = (
        jnp.einsum("ikgd,jkd->kgij", query_rows, key_row_slice, preferred_element_type=jnp.float32)
        * 0.125
    )
    query_pos = offset + jnp.arange(count_of_rows, dtype=jnp.int32)
    key_pos = offset - WINDOW_TOKENS + jnp.arange(WINDOW_TOKENS + count_of_rows, dtype=jnp.int32)
    distance = query_pos[:, None] - key_pos[None, :]
    inside = (distance >= 0) & (distance < WINDOW_TOKENS) & (key_pos >= 0)[None, :]
    head_sink_logit = attention_sink_logits[0].reshape(KEY_VALUE_HEADS, query_group_width)[
        :, :, None
    ]
    masked = jnp.where(inside, scores, -1e30)
    peak = jnp.maximum(jnp.max(masked, axis=-1), head_sink_logit)
    numer = jnp.where(inside, jnp.exp(masked - peak[..., None]), 0.0)
    denominator = jnp.sum(numer, axis=-1) + jnp.exp(head_sink_logit - peak)
    attention = (numer / denominator[..., None]).astype(jnp.bfloat16)
    mixed = jnp.einsum(
        "kgij,jkd->ikgd", attention, value_row_slice, preferred_element_type=jnp.float32
    )
    attended = mixed.astype(jnp.bfloat16).reshape(count_of_rows, QUERY_HEADS * HEAD_DIM)
    residual = (
        state.astype(jnp.float32)
        + jnp.dot(attended, out_weight[0], preferred_element_type=jnp.float32)
        + out_bias[0]
    ).astype(jnp.bfloat16)
    normed_mid = normed(residual, expert_gain[0])
    flat_ids = expert_ids[0].reshape(-1)
    expert_range = jnp.arange(experts_count, dtype=jnp.int32)
    one_hot = (flat_ids[:, None] == expert_range[None, :]).astype(jnp.int32)
    slot_of = jnp.sum((jnp.cumsum(one_hot, axis=0) - 1) * one_hot, axis=-1)
    token_of = jnp.arange(count_of_rows * TOP, dtype=jnp.int32) // TOP
    source_rows = (
        jnp.full((experts_count * slot_count,), -1, jnp.int32)
        .at[flat_ids * slot_count + slot_of]
        .set(token_of)
    )
    valid_rows = (source_rows >= 0)[:, None].astype(jnp.bfloat16)
    gathered = jnp.take(normed_mid, jnp.maximum(source_rows, 0), axis=0) * valid_rows
    by_expert = gathered.reshape(experts_count, slot_count, model_width)
    holders = placement[0]
    by_pair = jnp.take(by_expert, holders, axis=0)
    matches = (holders[:, None] == expert_range[None, :]).astype(jnp.int32)
    holder_of = jnp.sum(expert_range[:, None] * matches, axis=0)
    outgoing = jnp.repeat(by_pair, 2, axis=0)
    rows_in = lax.all_to_all(outgoing, "expert", split_axis=0, concat_axis=0, tiled=True)
    in_shape = rows_in.shape
    hidden = jnp.dot(rows_in.reshape(-1, model_width), tile_gu, preferred_element_type=jnp.float32)
    returned = lax.all_to_all(
        jnp.dot(swiglu(hidden), tile_down, preferred_element_type=jnp.float32)
        .astype(jnp.bfloat16)
        .reshape(in_shape),
        "expert",
        split_axis=0,
        concat_axis=0,
        tiled=True,
    )
    paired = returned.astype(jnp.float32).reshape(experts_count, 2, slot_count, model_width)
    summed = (
        (paired[:, 0] + paired[:, 1])
        .astype(jnp.bfloat16)
        .reshape(experts_count * slot_count, model_width)
    )
    picked = jnp.take(summed, holder_of[flat_ids] * slot_count + slot_of, axis=0).reshape(
        count_of_rows, TOP, model_width
    )
    picked = lax.optimization_barrier(picked).astype(jnp.float32)
    gate_weights = jax.nn.softmax(gate_logits[0], axis=-1)
    fresh = (
        residual.astype(jnp.float32) + jnp.sum(picked * gate_weights[..., None], axis=1)
    ).astype(jnp.bfloat16)
    moved = passed_along(fresh, "section", 1)
    return moved[None]


def solution(mesh):
    return jax.shard_map(
        shards,
        mesh=mesh,
        in_specs=(
            P("section", "expert", None),
            P("section", None),
            P("section", "expert", None),
            P("section", None),
            P("section", None, None),
            P("section", None),
            P("section", None),
            P("section", None),
            P("section", "expert", None, None),
            P("section", "expert", None, None),
            P("section", "expert", None),
            P("section", "expert", None),
            P("section", None),
        ),
        out_specs=P("section", "expert", None),
        check_vma=False,
    )
```

profile of v0, /device:TPU:1, one launch (start us, length us, event | category | flops | bytes accessed | tf_op | source)
XLA Modules:
  0.0 546.4 jit_solution(6834803989660928297)
XLA Ops:
  6.6 4.0 copy.62
  13.5 4.4 compare_select_fusion.4
  18.5 2.4 scatter_custom_fusion
  21.6 168.8 %all-gather.3.cloned.1.call-done = bf16[1,2880,2560]{2,0,1:T(2,128)(2,1)} async-done(((bf16[1,180,2560]{2,0,1:T(2,128)(2,1)}), bf16[1,2880,2560]{2,0,1:T(2,128)(2,1)}) %all-gather.3.cloned.1.call-update) | async-done | bytes 14745616 | tf_op jit(solution)/shard_map/all_gather | solution.py:65
  190.4 15.2 %fusion.17 = bf16[128,2560]{1,0:T(8,128)(2,1)S(1)} fusion(bf16[1,2880,2560]{2,0,1:T(2,128)(2,1)} %all-gather.3.cloned.1.call-done, bf16[1,128,2880]{1,2,0:T(8,128)(2,1)S(1)} %copy-done.2, f32[2880]{0:T(1024)S(1)} %reduce.1, f32[128]{0:T(128)S(1)} %add_rsqrt_fusion.1, f32[2560]{0:T(1024)S(1)} %reduce.2), kind=kOutput, calls=%fused_computation.29 | convolution fusion | flops 1889566720 | bytes 16160512 | tf_op jit(solution)/shard_map/dot_general | solution.py:63
  205.6 3.4 collective-permute-start
  216.7 3.3 multiply_reduce_fusion.1
  222.0 4.6 gather_fusion
  226.5 4.5 select_multiply_fusion
  231.0 4.9 gather_fusion.1
  235.9 2.5 broadcast_select_fusion
  238.9 91.5 %all_to_all.10 = bf16[16,80,2880]{2,1,0:T(8,128)(2,1)S(1)} all-to-all(bf16[16,80,2880]{2,1,0:T(8,128)(2,1)S(1)} %bitcast.119), channel_id=1, replica_groups=mesh['section'=8,'expert'=16] {'expert'}, dimensions={0} | all-to-all | bytes 14745600 | tf_op jit(solution)/shard_map/all_to_all | solution.py:126
  330.4 15.5 %fusion.5 = f32[1280,1440]{0,1:T(8,128)} fusion(bf16[1280,2880]{1,0:T(8,128)(2,1)S(1)} %bitcast.121, bf16[1,1,2880,1440]{2,3,1,0:T(8,128)(2,1)} %param.21), kind=kOutput, calls=%fused_computation.10 | convolution fusion | flops 10616832000 | bytes 23040000 | tf_op jit(solution)/shard_map/dot_general | solution.py:128
  345.9 11.9 %convolution_convert_fusion = bf16[1280,2880]{0,1:T(8,128)(2,1)} fusion(bf16[1,1,720,2880]{3,2,1,0:T(8,128)(2,1)S(1)} %bitcast.134, f32[1280,1440]{0,1:T(8,128)} %fusion.5), kind=kOutput, calls=%fused_computation.9 | convolution fusion | flops 5319475200 | bytes 18892800 | tf_op jit(solution)/shard_map/dot_general | solution.py:130
  357.8 10.4 %copy.71 = bf16[1280,2880]{1,0:T(8,128)(2,1)} copy(bf16[1280,2880]{0,1:T(8,128)(2,1)} %convolution_convert_fusion) | data formatting | bytes 14745600 | tf_op jit(solution)/shard_map/convert_element_type | solution.py:131
  368.3 4.8 all-to-all-start.1
  373.4 110.7 %all-to-all-done.1 = bf16[16,80,2880]{2,1,0:T(8,128)(2,1)} async-done(((bf16[16,80,2880]{2,1,0:T(8,128)(2,1)}), bf16[16,80,2880]{2,1,0:T(8,128)(2,1)}, u32[]{:S(2)}, u32[]{:S(2)}) %all-to-all-start.1) | async-done | bytes 7372832 | tf_op jit(solution)/shard_map/all_to_all | solution.py:129
  484.1 9.5 %convert.4 = f32[8,2,80,2880]{3,2,1,0:T(8,128)} convert(bf16[8,2,80,2880]{3,2,1,0:T(8,128)(2,1)} %bitcast.36) | non-fusion elementwise | flops 3686400 | bytes 22118400 | tf_op jit(solution)/shard_map/reshape | solution.py:138
  493.7 7.8 %fusion.8 = bf16[8,1,80,2880]{3,2,0,1:T(8,128)(2,1)} fusion(f32[8,2,80,2880]{3,2,1,0:T(8,128)} %convert.4), kind=kLoop, calls=%fused_computation.14 | loop fusion | flops 3686400 | bytes 18432000 | tf_op jit(solution)/shard_map/convert_element_type | solution.py:141
  501.5 9.3 %gather_fusion.2 = bf16[512,2880]{1,0:T(8,128)(2,1)} fusion(bf16[640,2880]{1,0:T(8,128)(2,1)} %bitcast.117, s32[1024]{0:T(1024)S(1)} %pad_clamp_fusion), kind=kCustom, calls=%fused_computation.2 | custom fusion | bytes 5900288 | tf_op jit(solution)/shard_map/jit(_take)/gather | solution.py:144
  510.7 4.9 gather.24
  517.1 4.5 multiply_reduce_fusion
  524.6 5.4 collective-permute-start.1
  530.0 8.4 %collective-permute-done.1 = bf16[128,2880]{0,1:T(8,128)(2,1)S(1)} collective-permute-done((bf16[128,2880]{0,1:T(8,128)(2,1)S(1)}, bf16[128,2880]{0,1:T(8,128)(2,1)S(1)}, u32[]{:S(2)}, u32[]{:S(2)}) %collective-permute-start.1) | collective-permute-done | bytes 737312 | tf_op jit(solution)/shard_map/ppermute | solution.py:21
  (100 shorter events, 19.8 us)
Async XLA Ops:
  6.5 4.0 copy-start.8
  6.5 4.5 copy-start.4
  6.5 4.5 copy-start.7
  6.5 6.0 %copy-start.9 = (s32[1,8]{1,0:T(1,128)S(1)}, s32[1,8]{1,0:T(1,128)}, u32[]{:S(2)}) copy-start(s32[1,8]{1,0:T(1,128)} %param.25) | copy-start | bytes 100
  6.5 14.5 %copy-start.2 = (bf16[1,128,2880]{1,2,0:T(8,128)(2,1)S(1)}, bf16[1,128,2880]{1,2,0:T(8,128)(2,1)}, u32[]{:S(2)}) copy-start(bf16[1,128,2880]{1,2,0:T(8,128)(2,1)} %param.13) | copy-start | bytes 2211844
  6.5 183.8 %all-gather.3.cloned.1.call-start = ((), (), s32[]{:S(2)}) async-start(), calls=%async_computation.2 | async-start | bytes 31334400 | tf_op jit(solution)/shard_map/all_gather | solution.py:65
  21.6 187.5 %copy-start.5 = (f32[1,2880]{1,0:T(1,128)S(1)}, f32[1,2880]{1,0:T(1,128)}, u32[]{:S(2)}) copy-start(f32[1,2880]{1,0:T(1,128)} %param.18) | copy-start | bytes 34564
  21.6 188.0 %copy-start.10 = (f32[1,32]{1,0:T(1,128)S(1)}, f32[1,32]{1,0:T(1,128)}, u32[]{:S(2)}) copy-start(f32[1,32]{1,0:T(1,128)} %param.19) | copy-start | bytes 388
  21.6 188.8 %copy-start.6 = (f32[1,2880]{1,0:T(1,128)S(1)}, f32[1,2880]{1,0:T(1,128)}, u32[]{:S(2)}) copy-start(f32[1,2880]{1,0:T(1,128)} %param.20) | copy-start | bytes 34564
  205.6 5.3 collective-permute-start
  212.1 2.5 slice-start
  213.2 2.5 slice-start.1
  213.2 3.5 slice-start.2
  220.0 1.2 copy-start
  238.9 107.0 %slice-start.3 = ((s8[4239360]{0:T(1024)(128)(4,1)}), s8[45056]{0:T(1024)(128)(4,1)S(1)}, s32[]{:S(2)}) async-start(s8[4239360]{0:T(1024)(128)(4,1)} %bitcast.133), calls=%async_computation.6 | async-start | bytes 90112
  330.4 15.5 %slice-start.4 = ((s8[4239360]{0:T(1024)(128)(4,1)}), s8[4194304]{0:T(1024)(128)(4,1)S(1)}, s32[]{:S(2)}) async-start(s8[4239360]{0:T(1024)(128)(4,1)} %bitcast.133), calls=%async_computation.7 | async-start | bytes 8388608
  368.3 5.0 copy-start.3
  368.3 115.9 %all-to-all-start.1 = ((bf16[16,80,2880]{2,1,0:T(8,128)(2,1)}), bf16[16,80,2880]{2,1,0:T(8,128)(2,1)}, u32[]{:S(2)}, u32[]{:S(2)}) async-start(bf16[16,80,2880]{2,1,0:T(8,128)(2,1)} %bitcast.118), calls=%async_computation.1 | async-start | bytes 15073280 | tf_op jit(solution)/shard_map/all_to_all | solution.py:129
  517.1 6.1 %copy-start.1 = (f32[128,2880]{0,1:T(8,128)S(1)}, f32[128,2880]{0,1:T(8,128)}, u32[]{:S(2)}) copy-start(f32[128,2880]{0,1:T(8,128)} %copy-done) | copy-start | bytes 4423684
  524.6 13.8 %collective-permute-start.1 = (bf16[128,2880]{0,1:T(8,128)(2,1)S(1)}, bf16[128,2880]{0,1:T(8,128)(2,1)S(1)}, u32[]{:S(2)}, u32[]{:S(2)}) collective-permute-start(bf16[128,2880]{0,1:T(8,128)(2,1)S(1)} %add_convert_fusion), channel_id=1, source_target_pairs={{0,16},{16,32},{32,48},{48,64},{64,80},{80,96},{96,112},{112,0},{1... | collective-permute-start | bytes 2211848 | tf_op jit(solution)/shard_map/ppermute | solution.py:21
Sparse Core Ops, SparseCore 0:
  10.7 179.6 all-gather.2
where the time goes:
time: 555 us; the launch traced here: 546 us
  waiting for transfers between devices  288 us (52%)
  blocking collectives  91.5 us (16%)
  local copies, waits for them, and re-layouts  50 us (9%)
  matrix products  47.9 us (9%)
  other arithmetic  41.3 us (7%)
  between operations  14.1 us (3%)
  starting transfers between devices  13.7 us (2%)
    all_gather x1, waiting for transfers between devices, shards(): lax.all_gather(query_key_value_weight[0], 'expert', axis=0, tiled=True)  169 us
    all_to_all x1, waiting for transfers between devices, shards(): lax.all_to_all(jnp.dot(swiglu(hidden), tile_down, preferred_element_type=...  111 us
    all_to_all x1, blocking collectives, shards(): lax.all_to_all(outgoing, 'expert', split_axis=0, concat_axis=0, tiled=True)  91.5 us
    dot_general x1, matrix products, shards(): jnp.dot(rows_in.reshape(-1, model_width), tile_gu, preferred_element_type...  15.5 us
    dot_general x1, matrix products, shards(): jnp.dot(normed_in, lax.all_gather(query_key_value_weight[0], 'expert', ax...  15.2 us
    gather x2, local copies, waits for them, and re-layouts, shards(): jnp.take(summed, holder_of[flat_ids] * slot_count + slot_of, axis=0)  14.1 us
    dot_general x1, matrix products, shards(): jnp.dot(swiglu(hidden), tile_down, preferred_element_type=jnp.float32)  11.9 us
  transfers between devices with their start and end apart: 4, of which 3 were waited for; matrix products, arithmetic and copies ran while one was open for 2% of the time, Pallas kernels for 0%

commit v1 on v0

v1 whole, which is shorter than its diff:
```python
import functools

import jax
import jax.numpy as jnp
from jax import lax
from jax.experimental import pallas as pl
from jax.experimental.pallas import tpu as pltpu
from jax.sharding import PartitionSpec as P

HEAD_DIM = 64
QUERY_HEADS = 32
KEY_VALUE_HEADS = 4
WINDOW_TOKENS = 128
TOP = 4
SIDE = 4
MESH = pl.DeviceIdType.MESH
F32 = jnp.float32
BF16 = jnp.bfloat16


def from_behind(x, axis, by):
    size = lax.axis_size(axis)
    pairs = [(i, i + by) for i in range(size) if 0 <= i + by < size]
    return lax.ppermute(x, axis, pairs)


def normed(vector, gain_row):
    as_float = vector.astype(jnp.float32)
    inverse_rms = lax.rsqrt(jnp.mean(as_float * as_float, axis=-1, keepdims=True) + 1e-05)
    return (as_float * inverse_rms * gain_row).astype(jnp.bfloat16)


class Links:
    def __init__(self, send, recv):
        self.send, self.recv = send, recv
        self.keys, self.started, self.done = {}, [], set()
        self.made = {}
        self.section = lax.axis_index("section")
        me = lax.axis_index("expert")
        self.x, self.z = me // SIDE, me % SIDE

    def neighbour(self, axis, step):
        if axis == 2:
            return ((self.section + step + 8) % 8, self.x * SIDE + self.z)
        if axis == 0:
            return (self.section, ((self.x + step + SIDE) % SIDE) * SIDE + self.z)
        return (self.section, self.x * SIDE + (self.z + step + SIDE) % SIDE)

    def barrier(self, partners):
        sem = pltpu.get_barrier_semaphore()
        for axis, step in partners:
            pl.semaphore_signal(
                sem, inc=1, device_id=self.neighbour(axis, step), device_id_type=MESH
            )
        pl.semaphore_wait(sem, len(partners))

    def start(self, name, src, dst, axis, step):
        key = self.keys.setdefault(name, len(self.keys))
        copy = pltpu.make_async_remote_copy(
            src_ref=src(),
            dst_ref=dst(),
            send_sem=self.send.at[key],
            recv_sem=self.recv.at[key],
            device_id=self.neighbour(axis, step),
            device_id_type=MESH,
        )
        copy.start()
        self.made[name] = (src, dst, axis, step)

    def remake(self, name):
        src, dst, axis, step = self.made[name]
        key = self.keys[name]
        return pltpu.make_async_remote_copy(
            src_ref=src(),
            dst_ref=dst(),
            send_sem=self.send.at[key],
            recv_sem=self.recv.at[key],
            device_id=self.neighbour(axis, step),
            device_id_type=MESH,
        )

    def need(self, *names):
        for name in names:
            if name not in self.done:
                self.done.add(name)
                self.remake(name).wait_recv()

    def finish(self):
        for name in self.made:
            self.need(name)
            self.remake(name).wait_send()


def add_rows(dst, *parts):
    step = 16

    def body(i, carry):
        rows = pl.ds(pl.multiple_of(i * step, step), step)
        total = parts[0][rows].astype(F32)
        for part in parts[1:]:
            total = total + part[rows].astype(F32)
        dst[rows] = total.astype(dst.dtype)
        return carry

    lax.fori_loop(0, dst.shape[0] // step, body, 0)


def view(ref, *index):
    return lambda: ref.at[index]


def chunks(total, size):
    return [(at, min(size, total - at)) for at in range(0, total, size)]


def expert_kernel(
    slots,
    normed_ref,
    residual_ref,
    meta_ref,
    chosen_ref,
    gate_up_hbm,
    down_hbm,
    out_ref,
    tokens,
    parts,
    meta,
    gate_up,
    down,
    packed,
    hidden,
    act,
    picks,
    half_in,
    full_in,
    half_last,
    full_last,
    local_sem,
    send_sem,
    recv_sem,
):
    half_rows = tokens.shape[2] // 2
    quarter = half_rows // 2
    width = tokens.shape[3]
    inner = act.shape[1]
    net = Links(send_sem, recv_sem)
    load_tokens = pltpu.make_async_copy(normed_ref, tokens.at[0, 0], local_sem.at[0])
    load_gate_up = pltpu.make_async_copy(gate_up_hbm, gate_up, local_sem.at[1])
    load_down = pltpu.make_async_copy(down_hbm, down, local_sem.at[2])
    load_tokens.start()
    meta[0, 0] = meta_ref[...]
    net.barrier([(0, 1), (0, -1), (1, 1), (1, -1), (2, 1), (2, -1)])

    net.start(("mx", 1), view(meta, 0, 0), view(meta, 0, 3), 0, 1)
    net.start(("mx", -1), view(meta, 0, 0), view(meta, 0, 1), 0, -1)
    load_tokens.wait()
    load_gate_up.start()
    load_down.start()

    def block(which, dp, dq, at, size):
        first, second = (dp, dq) if which == 0 else (dq, dp)
        rows = slice(which * half_rows + at, which * half_rows + at + size)
        return lambda: tokens.at[first, second, rows]

    def part(which, dp, dq, at, size):
        first, second = (dp, dq) if which == 0 else (dq, dp)
        rows = slice(which * half_rows + at, which * half_rows + at + size)
        return lambda: parts.at[first, second, rows]

    def own(which, axis, step):
        to = (-step) % SIDE
        place = (to, 0) if axis == which else (0, to)
        name = ("op" if axis == which else "oq", which, step)
        net.start(
            name,
            block(which, 0, 0, 0, half_rows),
            block(which, *place, 0, half_rows),
            axis,
            step,
        )

    for axis in (0, 1):
        for step in (1, -1):
            own(axis, axis, step)
    for axis in (0, 1):
        for step in (1, -1):
            own(1 - axis, axis, step)
    net.need(("mx", 1))
    net.start(("mf", 0), view(meta, 0, 3), view(meta, 0, 2), 0, 1)

    def at_of(step):
        return 0 if step == 1 else quarter

    def on_across(which, dp, dq_axis_step):
        step = dq_axis_step
        net.start(
            ("pq", which, dp, step),
            block(which, dp, 0, 0, half_rows),
            block(which, dp, (-step) % SIDE, 0, half_rows),
            1 - which,
            step,
        )

    def first_hops():
        for step in (1, -1):
            for which in (0, 1):
                dp = (-step) % SIDE
                net.need(("op", which, step))
                net.start(
                    ("fp", which, step),
                    block(which, dp, 0, at_of(step), quarter),
                    block(which, 2, 0, at_of(step), quarter),
                    which,
                    step,
                )
                on_across(which, dp, 1)
                on_across(which, dp, -1)

    def meta_across():
        net.need(("mx", -1), ("mf", 0))
        net.start(("mz", 1), view(meta, 0), view(meta, 3), 1, 1)
        net.start(("mz", -1), view(meta, 0), view(meta, 1), 1, -1)

    def meta_last():
        net.need(("mz", 1), ("mz", -1))
        net.start(("mg", 0), view(meta, 3), view(meta, 2), 1, 1)

    def far_hops():
        for half in (1, -1):
            for which in (0, 1):
                net.need(("fp", which, half))
                for step in (1, -1):
                    net.start(
                        ("pq2", which, half, step),
                        block(which, 2, 0, at_of(half), quarter),
                        block(which, 2, (-step) % SIDE, at_of(half), quarter),
                        1 - which,
                        step,
                    )

    def second_hops(dp):
        for step in (1, -1):
            for which in (0, 1):
                if dp == 0:
                    net.need(("oq", which, step))
                elif dp == 2:
                    net.need(("pq2", which, step, step))
                else:
                    net.need(("pq", which, dp, step))
                net.start(
                    ("fq", which, dp, step),
                    block(which, dp, (-step) % SIDE, at_of(step), quarter),
                    block(which, dp, 2, at_of(step), quarter),
                    1 - which,
                    step,
                )

    def arrived(dx):
        for dz in range(SIDE):
            for which in (0, 1):
                dp, dq = (dx, dz) if which == 0 else (dz, dx)
                step = {1: -1, 3: 1}
                if dq == 0:
                    if dp in step:
                        net.need(("op", which, step[dp]))
                    elif dp == 2:
                        net.need(("fp", which, 1), ("fp", which, -1))
                elif dq == 2:
                    net.need(("fq", which, dp, 1), ("fq", which, dp, -1))
                elif dp == 0:
                    net.need(("oq", which, step[dq]))
                elif dp == 2:
                    net.need(("pq2", which, 1, step[dq]), ("pq2", which, -1, step[dq]))
                else:
                    net.need(("pq", which, dp, step[dq]))

    def stage(at):
        if at == 0:
            meta_across()
            first_hops()
            meta_last()
            far_hops()
            second_hops(0)
            net.need(("mg", 0))
            load_gate_up.wait()
            load_down.wait()
            arrived(0)
        elif at == 1:
            second_hops(1)
            second_hops(3)
            arrived(1)
        elif at == 2:
            second_hops(2)
            arrived(3)
        else:
            arrived(2)

    before = lax.broadcasted_iota(jnp.int32, (128, 128), 0)
    after = lax.broadcasted_iota(jnp.int32, (128, 128), 1)
    earlier = jnp.where(before < after, 1.0, 0.0).astype(BF16)
    slot = lax.broadcasted_iota(jnp.int32, (slots, 128), 0).astype(F32)

    def group(g, carry):
        for at in range(SIDE):
            pl.when(g == at)(functools.partial(stage, at))
        dx = g + g // 2 - 2 * (g // 3)
        scales = []
        for dz in range(SIDE):
            table = meta[dz, dx]
            member = jnp.sum(table[0:8] * chosen_ref[...], axis=0, keepdims=True)
            weight = jnp.sum(table[8:16] * chosen_ref[...], axis=0, keepdims=True)
            wide = jnp.broadcast_to(member, (16, 128)).astype(BF16)
            rank = jnp.dot(wide, earlier, preferred_element_type=F32)[0:1]
            hit = (slot == rank) & (member > 0.5)
            pick = jnp.where(hit, 1.0, 0.0).astype(BF16)
            scales.append(jnp.sum(jnp.where(hit, weight, 0.0), axis=1, keepdims=True))
            picks[dz] = pick
            for at, size in chunks(width, 1024):
                packed[dz * slots : (dz + 1) * slots, at : at + size] = jnp.dot(
                    pick, tokens[dx, dz, :, at : at + size], preferred_element_type=F32
                ).astype(BF16)
        scale = jnp.concatenate(scales, axis=0)
        for at, size in chunks(2 * inner, 512):
            hidden[:, at : at + size] = jnp.dot(
                packed[...], gate_up[:, at : at + size], preferred_element_type=F32
            )
        gate = hidden[:, :inner]
        up = hidden[:, inner:]
        act[...] = ((up + 1.0) * gate * jax.nn.sigmoid(1.702 * gate)).astype(BF16)
        for at, size in chunks(width, 640):
            tile = jnp.dot(act[...], down[:, at : at + size], preferred_element_type=F32)
            tile = (tile * scale).astype(BF16)
            for dz in range(SIDE):
                parts[dx, dz, :, at : at + size] = lax.dot_general(
                    picks[dz],
                    tile[dz * slots : (dz + 1) * slots],
                    (((0,), (0,)), ((), ())),
                    preferred_element_type=F32,
                ).astype(BF16)
        return carry

    lax.fori_loop(0, SIDE, group, 0)

    for dp in (2, 1, 3, 0):
        for which in (0, 1):
            for side, step in ((0, 1), (1, -1)):
                net.start(
                    ("rh", which, dp, step),
                    part(which, dp, 2, at_of(step), quarter),
                    view(half_in, which, dp, side),
                    1 - which,
                    step,
                )

    def relay(dp):
        for which in (0, 1):
            for side, step in ((0, 1), (1, -1)):
                net.need(("rh", which, dp, step))
                there = part(which, dp, step % SIDE, at_of(step), quarter)
                add_rows(there(), there(), half_in.at[which, dp, side])
                net.start(
                    ("rf", which, dp, step),
                    part(which, dp, step % SIDE, 0, half_rows),
                    view(full_in, which, dp, side),
                    1 - which,
                    step,
                )

    def gather_in(dp):
        for which in (0, 1):
            net.need(("rf", which, dp, 1), ("rf", which, dp, -1))
            here = part(which, dp, 0, 0, half_rows)
            add_rows(here(), here(), full_in.at[which, dp, 0], full_in.at[which, dp, 1])

    def last_half(which):
        for side, step in ((0, 1), (1, -1)):
            net.start(
                ("lh", which, step),
                part(which, 2, 0, at_of(step), quarter),
                view(half_last, which, side),
                which,
                step,
            )

    def last_full(which):
        for side, step in ((0, 1), (1, -1)):
            net.need(("lh", which, step))
            there = part(which, step % SIDE, 0, at_of(step), quarter)
            add_rows(there(), there(), half_last.at[which, side])
            net.start(
                ("lf", which, step),
                part(which, step % SIDE, 0, 0, half_rows),
                view(full_last, which, side),
                which,
                step,
            )

    relay(2)
    relay(1)
    gather_in(2)
    last_half(0)
    last_half(1)
    relay(3)
    gather_in(1)
    relay(0)
    gather_in(3)
    last_full(0)
    last_full(1)
    for which in (0, 1):
        net.need(("rf", which, 0, 1), ("rf", which, 0, -1))
        net.need(("lf", which, 1), ("lf", which, -1))
        here = part(which, 0, 0, 0, half_rows)
        rows = slice(which * half_rows, (which + 1) * half_rows)
        add_rows(
            here(),
            here(),
            full_in.at[which, 0, 0],
            full_in.at[which, 0, 1],
            full_last.at[which, 0],
            full_last.at[which, 1],
            residual_ref.at[rows],
        )
        net.start(("out", which), here, view(out_ref, rows), 2, 1)
    net.finish()


def experts_and_pass(normed_mid, residual, meta, chosen, gate_up, down, slots):
    rows, width = normed_mid.shape
    inner = down.shape[0]
    anywhere = pl.BlockSpec(memory_space=pl.ANY)
    vmem = pl.BlockSpec(memory_space=pltpu.VMEM)
    half, quarter = rows // 2, rows // 4
    return pl.pallas_call(
        functools.partial(expert_kernel, slots),
        out_shape=jax.ShapeDtypeStruct((rows, width), BF16),
        in_specs=[anywhere, vmem, vmem, vmem, anywhere, anywhere],
        out_specs=anywhere,
        scratch_shapes=[
            pltpu.VMEM((SIDE, SIDE, rows, width), BF16),
            pltpu.VMEM((SIDE, SIDE, rows, width), BF16),
            pltpu.VMEM((SIDE, SIDE, 16, rows), F32),
            pltpu.VMEM(gate_up.shape, BF16),
            pltpu.VMEM(down.shape, BF16),
            pltpu.VMEM((SIDE * slots, width), BF16),
            pltpu.VMEM((SIDE * slots, 2 * inner), F32),
            pltpu.VMEM((SIDE * slots, inner), BF16),
            pltpu.VMEM((SIDE, slots, rows), BF16),
            pltpu.VMEM((2, SIDE, 2, quarter, width), BF16),
            pltpu.VMEM((2, SIDE, 2, half, width), BF16),
            pltpu.VMEM((2, 2, quarter, width), BF16),
            pltpu.VMEM((2, 2, half, width), BF16),
            pltpu.SemaphoreType.DMA((3,)),
            pltpu.SemaphoreType.DMA((96,)),
            pltpu.SemaphoreType.DMA((96,)),
        ],
        compiler_params=pltpu.CompilerParams(
            collective_id=1, has_side_effects=True, vmem_limit_bytes=62 * 1024 * 1024
        ),
        cost_estimate=pl.CostEstimate(
            flops=16_000_000_000, bytes_accessed=16_000_000, transcendentals=1_000_000
        ),
    )(normed_mid, residual, meta, chosen, gate_up, down)


def routing_tables(ids, logits, holders):
    kinds = lax.broadcasted_iota(jnp.int32, (8, ids.shape[0], TOP), 0)
    equal = (ids[None] == kinds).astype(F32)
    weights = jax.nn.softmax(logits, axis=-1)
    member = jnp.sum(equal, axis=-1)
    weight = jnp.sum(equal * weights[None], axis=-1)
    pair = lax.axis_index("expert") // 2
    mine = jnp.sum(jnp.where(jnp.arange(8) == pair, holders, 0))
    chosen = (lax.broadcasted_iota(jnp.int32, (8, ids.shape[0]), 0) == mine).astype(F32)
    return jnp.concatenate([member, weight], axis=0), chosen


def shards(
    section_input,
    attention_gain,
    query_key_value_weight,
    qkv_bias,
    out_weight,
    out_bias,
    attention_sink_logits,
    expert_gain,
    gate_up_weight,
    down_weight,
    expert_ids,
    gate_logits,
    placement,
):
    count_of_rows = section_input.shape[1]
    experts_count = placement.shape[1]
    slots = 2 * min(count_of_rows // 2, count_of_rows * TOP * 5 // (8 * experts_count))
    offset = lax.axis_index("expert") * count_of_rows
    query_group_width = QUERY_HEADS // KEY_VALUE_HEADS
    state = section_input[0]
    normed_in = normed(state, attention_gain[0])
    projected_rows = (
        jnp.dot(
            normed_in,
            lax.all_gather(query_key_value_weight[0], "expert", axis=0, tiled=True),
            preferred_element_type=jnp.float32,
        )
        + qkv_bias[0]
    ).astype(jnp.bfloat16)
    query_rows = projected_rows[:, : QUERY_HEADS * HEAD_DIM].reshape(
        count_of_rows, KEY_VALUE_HEADS, query_group_width, HEAD_DIM
    )
    key_value = projected_rows[:, QUERY_HEADS * HEAD_DIM :]
    rim_rows = from_behind(key_value, "expert", 1)
    rows_in_window = jnp.concatenate([rim_rows, key_value], 0)
    key_row_slice = rows_in_window[:, : KEY_VALUE_HEADS * HEAD_DIM].reshape(
        WINDOW_TOKENS + count_of_rows, KEY_VALUE_HEADS, HEAD_DIM
    )
    value_row_slice = rows_in_window[:, KEY_VALUE_HEADS * HEAD_DIM :].reshape(
        WINDOW_TOKENS + count_of_rows, KEY_VALUE_HEADS, HEAD_DIM
    )
    scores = (
        jnp.einsum("ikgd,jkd->kgij", query_rows, key_row_slice, preferred_element_type=jnp.float32)
        * 0.125
    )
    query_pos = offset + jnp.arange(count_of_rows, dtype=jnp.int32)
    key_pos = offset - WINDOW_TOKENS + jnp.arange(WINDOW_TOKENS + count_of_rows, dtype=jnp.int32)
    distance = query_pos[:, None] - key_pos[None, :]
    inside = (distance >= 0) & (distance < WINDOW_TOKENS) & (key_pos >= 0)[None, :]
    head_sink_logit = attention_sink_logits[0].reshape(KEY_VALUE_HEADS, query_group_width)[
        :, :, None
    ]
    masked = jnp.where(inside, scores, -1e30)
    peak = jnp.maximum(jnp.max(masked, axis=-1), head_sink_logit)
    numer = jnp.where(inside, jnp.exp(masked - peak[..., None]), 0.0)
    denominator = jnp.sum(numer, axis=-1) + jnp.exp(head_sink_logit - peak)
    attention = (numer / denominator[..., None]).astype(jnp.bfloat16)
    mixed = jnp.einsum(
        "kgij,jkd->ikgd", attention, value_row_slice, preferred_element_type=jnp.float32
    )
    attended = mixed.astype(jnp.bfloat16).reshape(count_of_rows, QUERY_HEADS * HEAD_DIM)
    residual = (
        state.astype(jnp.float32)
        + jnp.dot(attended, out_weight[0], preferred_element_type=jnp.float32)
        + out_bias[0]
    ).astype(jnp.bfloat16)
    normed_mid = normed(residual, expert_gain[0])
    meta, chosen = routing_tables(expert_ids[0], gate_logits[0], placement[0])
    moved = experts_and_pass(
        normed_mid, residual, meta, chosen, gate_up_weight[0, 0], down_weight[0, 0], slots
    )
    return moved[None]


def solution(mesh):
    return jax.shard_map(
        shards,
        mesh=mesh,
        in_specs=(
            P("section", "expert", None),
            P("section", None),
            P("section", "expert", None),
            P("section", None),
            P("section", None, None),
            P("section", None),
            P("section", None),
            P("section", None),
            P("section", "expert", None, None),
            P("section", "expert", None, None),
            P("section", "expert", None),
            P("section", "expert", None),
            P("section", None),
        ),
        out_specs=P("section", "expert", None),
        check_vma=False,
    )
```

time: 555 us -> 407 us (0.73)
  Pallas kernels: 0 us -> 160 us
  waiting for transfers between devices: 288 us -> 178 us
  blocking collectives: 91.5 us -> 0 us
  other arithmetic: 41.3 us -> 5.56 us
  matrix products: 47.9 us -> 18 us
  local copies, waits for them, and re-layouts: 50 us -> 22.3 us
  starting transfers between devices: 13.7 us -> 3.18 us
    pallas_call x0 -> x1, Pallas kernels: none -> 160 us  [experts_and_pass(): pl.pallas_call(functools.partial(expert_kernel, slots), out_shape=jax.Sha...]
    all_to_all x1 -> x0, waiting for transfers between devices: 111 us -> none  [shards(): lax.all_to_all(jnp.dot(swiglu(hidden), tile_down, preferred_element_type=...]
    all_to_all x1 -> x0, blocking collectives: 91.5 us -> none  [shards(): lax.all_to_all(outgoing, 'expert', split_axis=0, concat_axis=0, tiled=True)]
    dot_general x2 -> x0, matrix products: 27.4 us -> none  [the longest x1 15.5 us: shards(): jnp.dot(rows_in.reshape(-1, model_width), tile_gu, preferred_element_type...]
    gather x5 -> x0, local copies, waits for them, and re-layouts: 24.3 us -> none  [the longest x2 14.1 us: shards(): jnp.take(summed, holder_of[flat_ids] * slot_count + slot_of, axis=0)]
    convert_element_type x2 -> x0, local copies, waits for them, and re-layouts: 10.8 us -> none  [the longest x1 10.4 us: shards(): returned = lax.all_to_all(jnp.dot(swiglu(hidden), tile_down, preferred_el...]
    unnamed x36 -> x30, local copies, waits for them, and re-layouts: 8.84 us -> 18.8 us
    reshape x1 -> x0, other arithmetic: 9.55 us -> none  [shards(): returned.astype(jnp.float32)]
  transfers between devices with their start and end apart: 4 -> 2, of which waited for: 3 -> 1; matrix products, arithmetic and copies ran while one was open for 2% -> 4% of each run, Pallas kernels for 0% -> 0%
where the time goes in v1:
time: 407 us; the launch traced here: 401 us
  waiting for transfers between devices  178 us (44%)
  Pallas kernels  160 us (39%)
  local copies, waits for them, and re-layouts  22.3 us (5%)
  matrix products  18 us (4%)
  between operations  13.7 us (3%)
  other arithmetic  5.56 us (1%)
    all_gather x1, waiting for transfers between devices, shards(): lax.all_gather(query_key_value_weight[0], 'expert', axis=0, tiled=True)  178 us
    pallas_call x1, Pallas kernels, experts_and_pass(): pl.pallas_call(functools.partial(expert_kernel, slots), out_shape=jax.Sha...  160 us
    unnamed x30, local copies, waits for them, and re-layouts  18.8 us
    dot_general x1, matrix products, shards(): jnp.dot(normed_in, lax.all_gather(query_key_value_weight[0], 'expert', ax...  11.7 us
  transfers between devices with their start and end apart: 2, of which 1 were waited for; matrix products, arithmetic and copies ran while one was open for 4% of the time, Pallas kernels for 0%

profile of v1, /device:TPU:1, one launch (start us, length us, event | category | flops | bytes accessed | tf_op | source)
XLA Modules:
  0.0 400.7 jit_solution(63728490982430023)
XLA Ops:
  6.6 3.9 copy.57
  10.6 0.4 copy.56
  11.1 0.6 fusion.39
  11.8 0.2 fusion.26
  12.1 0.1 fusion.36
  12.2 178.2 %all-gather.3.cloned.1.call-done = bf16[1,2880,2560]{2,0,1:T(2,128)(2,1)} async-done(((bf16[1,180,2560]{2,0,1:T(2,128)(2,1)}), bf16[1,2880,2560]{2,0,1:T(2,128)(2,1)}) %all-gather.3.cloned.1.call-update) | async-done | bytes 14745616 | tf_op jit(solution)/shard_map/all_gather | solution.py:502
  190.4 11.7 %fusion.18 = bf16[128,2560]{1,0:T(8,128)(2,1)S(1)} fusion(bf16[1,2880,2560]{2,0,1:T(2,128)(2,1)} %all-gather.3.cloned.1.call-done, bf16[1,128,2880]{2,1,0:T(8,128)(2,1)S(1)} %copy.56, f32[2880]{0:T(1024)S(1)} %reduce.1, f32[128]{0:T(128)S(1)} %add_rsqrt_fusion.1, f32[2560]{0:T(1024)S(1)} %reduce.2), kind=kOutput, calls=%fused_computation.13 | convolution fusion | flops 1889566720 | bytes 16160512 | tf_op jit(solution)/shard_map/dot_general | solution.py:500
  202.1 3.1 collective-permute-start
  205.3 0.7 compare_convert_fusion
  206.0 0.5 broadcast.84
  206.5 0.7 reduce.8
  207.3 11.7 %copy.63 = bf16[1,1,2880,1440]{3,2,1,0:T(8,128)(2,1)} copy(bf16[1,1,2880,1440]{2,3,1,0:T(8,128)(2,1)} %param.21) | data formatting | bytes 16588800 | tf_op args[8]
  219.0 0.6 pad_maximum_fusion.1.meta_ref
  219.7 0.3 copy.60
  220.2 0.8 fusion.8
  221.0 1.0 fusion.21
  222.2 1.3 fusion.29
  223.5 1.2 slice-done.1
  224.7 1.0 slice-done.2
  225.7 4.3 %fusion.23 = (f32[128]{0:T(128)S(1)}, bf16[128,2880]{1,0:T(8,128)(2,1)S(1)}) fusion(f32[2880]{0:T(1024)S(1)} %reduce.4, bf16[128,2048]{0,1:T(8,128)(2,1)S(1)} %bitcast.76, bf16[1,2048,2880]{1,2,0:T(8,128)(2,1)S(1)} %bitcast.72, bf16[1,128,2880]{2,1,0:T(8,128)(2,1)S(1)} %copy.56), kind=kOutput, calls=%fused_computation.20 | convolution fusion | flops 1512529792 | bytes 13807360 | tf_op jit(solution)/shard_map/dot_general | solution.py:541
  230.0 1.2 fusion.25.normed_ref
  231.2 0.7 iota.31.chosen_ref
  231.9 159.7 %shard_map.127 = bf16[128,2880]{1,0:T(8,128)(2,1)} custom-call(bf16[128,2880]{1,0:T(8,128)(2,1)} %fusion.25.normed_ref, bf16[128,2880]{1,0:T(8,128)(2,1)} %copy-done, f32[16,128]{1,0:T(8,128)} %pad_maximum_fusion.1.meta_ref, f32[8,128]{1,0:T(8,128)} %iota.31.chosen_ref, bf16[2880,1440]{1,0:T(8,128)(2,1)} %bitcast.73, bf16[720,2880]{1,0:T(8,128)(2,1)} %bitcast.80), custom_call_target="tpu_custom_call" | custom-call | flops 16000000000 | bytes 16000000 | tf_op jit(solution)/shard_map/pallas_call | solution.py:433
  391.6 2.3 copy.64
  (49 shorter events, 0.8 us)
Async XLA Ops:
  6.5 4.0 %copy-start.1 = (bf16[1,128,2880]{1,2,0:T(8,128)(2,1)S(1)}, bf16[1,128,2880]{1,2,0:T(8,128)(2,1)}, u32[]{:S(2)}) copy-start(bf16[1,128,2880]{1,2,0:T(8,128)(2,1)} %param.13) | copy-start | bytes 2211844
  6.5 4.4 %copy-start.3 = (f32[1,2880]{1,0:T(1,128)S(1)}, f32[1,2880]{1,0:T(1,128)}, u32[]{:S(2)}) copy-start(f32[1,2880]{1,0:T(1,128)} %param.14) | copy-start | bytes 34564
  6.5 4.5 %copy-start.6 = (f32[1,2560]{1,0:T(1,128)S(1)}, f32[1,2560]{1,0:T(1,128)}, u32[]{:S(2)}) copy-start(f32[1,2560]{1,0:T(1,128)} %param.16) | copy-start | bytes 30724
  6.5 4.5 %copy-start.2 = (f32[1,128,4]{1,2,0:T(4,128)S(1)}, f32[1,128,4]{1,2,0:T(4,128)}, u32[]{:S(2)}) copy-start(f32[1,128,4]{1,2,0:T(4,128)} %param.24) | copy-start | bytes 6148
  6.5 4.6 %copy-start.8 = (s32[1,8]{1,0:T(1,128)S(1)}, s32[1,8]{1,0:T(1,128)}, u32[]{:S(2)}) copy-start(s32[1,8]{1,0:T(1,128)} %param.25) | copy-start | bytes 100
  6.5 5.2 %copy-start.7 = (s32[1,128,4]{1,2,0:T(4,128)S(1)}, s32[1,128,4]{1,2,0:T(4,128)}, u32[]{:S(2)}) copy-start(s32[1,128,4]{1,2,0:T(4,128)} %param.23) | copy-start | bytes 6148
  6.6 183.8 %all-gather.3.cloned.1.call-start = ((), (), s32[]{:S(2)}) async-start(), calls=%async_computation | async-start | bytes 31334400 | tf_op jit(solution)/shard_map/all_gather | solution.py:502
  12.2 193.7 %copy-start.4 = (f32[1,2880]{1,0:T(1,128)S(1)}, f32[1,2880]{1,0:T(1,128)}, u32[]{:S(2)}) copy-start(f32[1,2880]{1,0:T(1,128)} %param.18) | copy-start | bytes 34564
  12.2 194.3 %copy-start.9 = (f32[1,32]{1,0:T(1,128)S(1)}, f32[1,32]{1,0:T(1,128)}, u32[]{:S(2)}) copy-start(f32[1,32]{1,0:T(1,128)} %param.19) | copy-start | bytes 388
  12.2 195.0 %copy-start.5 = (f32[1,2880]{1,0:T(1,128)S(1)}, f32[1,2880]{1,0:T(1,128)}, u32[]{:S(2)}) copy-start(f32[1,2880]{1,0:T(1,128)} %param.20) | copy-start | bytes 34564
  202.1 17.8 %collective-permute-start = (bf16[128,512]{1,0:T(8,128)(2,1)S(1)}, bf16[128,512]{1,0:T(8,128)(2,1)S(1)}, u32[]{:S(2)}, u32[]{:S(2)}) collective-permute-start(bf16[128,512]{1,0:T(8,128)(2,1)S(1)} %slice.16), channel_id=1, source_target_pairs={{0,1},{1,2},{2,3},{3,4},{4,5},{5,6},{6,7},{7,8},{8,9},{9,10},{10,1... | collective-permute-start | bytes 393224 | tf_op jit(solution)/shard_map/ppermute | solution.py:24
  221.0 2.4 slice-start
  222.2 2.6 slice-start.1
  222.2 3.5 slice-start.2
  230.0 1.9 copy-start
Sparse Core Ops, SparseCore 0:
  10.7 179.6 all-gather.2

commit v2 on v1

--- a/solution.py
+++ b/solution.py
@@ -18,12 +18,6 @@
 BF16 = jnp.bfloat16
 
 
-def from_behind(x, axis, by):
-    size = lax.axis_size(axis)
-    pairs = [(i, i + by) for i in range(size) if 0 <= i + by < size]
-    return lax.ppermute(x, axis, pairs)
-
-
 def normed(vector, gain_row):
     as_float = vector.astype(jnp.float32)
     inverse_rms = lax.rsqrt(jnp.mean(as_float * as_float, axis=-1, keepdims=True) + 1e-05)
@@ -40,6 +34,8 @@
         self.x, self.z = me // SIDE, me % SIDE
 
     def neighbour(self, axis, step):
+        if axis == 3:
+            return (self.section, (self.x * SIDE + self.z + step + 16) % 16)
         if axis == 2:
             return ((self.section + step + 8) % 8, self.x * SIDE + self.z)
         if axis == 0:
@@ -109,6 +105,14 @@
     return lambda: ref.at[index]
 
 
+def across(rows, other):
+    return lax.dot_general(rows, other, (((1,), (1,)), ((), ())), preferred_element_type=F32)
+
+
+def along(first, second):
+    return lax.dot_general(first, second, (((0,), (0,)), ((), ())), preferred_element_type=F32)
+
+
 def chunks(total, size):
     return [(at, min(size, total - at)) for at in range(0, total, size)]
 
@@ -124,11 +128,9 @@
     out_ref,
     tokens,
     parts,
-    meta,
     gate_up,
     down,
     packed,
-    hidden,
     act,
     picks,
     half_in,
@@ -148,11 +150,8 @@
     load_gate_up = pltpu.make_async_copy(gate_up_hbm, gate_up, local_sem.at[1])
     load_down = pltpu.make_async_copy(down_hbm, down, local_sem.at[2])
     load_tokens.start()
-    meta[0, 0] = meta_ref[...]
     net.barrier([(0, 1), (0, -1), (1, 1), (1, -1), (2, 1), (2, -1)])
 
-    net.start(("mx", 1), view(meta, 0, 0), view(meta, 0, 3), 0, 1)
-    net.start(("mx", -1), view(meta, 0, 0), view(meta, 0, 1), 0, -1)
     load_tokens.wait()
     load_gate_up.start()
     load_down.start()
@@ -185,8 +184,6 @@
     for axis in (0, 1):
         for step in (1, -1):
             own(1 - axis, axis, step)
-    net.need(("mx", 1))
-    net.start(("mf", 0), view(meta, 0, 3), view(meta, 0, 2), 0, 1)
 
     def at_of(step):
         return 0 if step == 1 else quarter
@@ -215,15 +212,6 @@
                 )
                 on_across(which, dp, 1)
                 on_across(which, dp, -1)
-
-    def meta_across():
-        net.need(("mx", -1), ("mf", 0))
-        net.start(("mz", 1), view(meta, 0), view(meta, 3), 1, 1)
-        net.start(("mz", -1), view(meta, 0), view(meta, 1), 1, -1)
-
-    def meta_last():
-        net.need(("mz", 1), ("mz", -1))
-        net.start(("mg", 0), view(meta, 3), view(meta, 2), 1, 1)
 
     def far_hops():
         for half in (1, -1):
@@ -276,12 +264,9 @@
 
     def stage(at):
         if at == 0:
-            meta_across()
             first_hops()
-            meta_last()
             far_hops()
             second_hops(0)
-            net.need(("mg", 0))
             load_gate_up.wait()
             load_down.wait()
             arrived(0)
@@ -306,7 +291,7 @@
         dx = g + g // 2 - 2 * (g // 3)
         scales = []
         for dz in range(SIDE):
-            table = meta[dz, dx]
+            table = meta_ref[dz, dx]
             member = jnp.sum(table[0:8] * chosen_ref[...], axis=0, keepdims=True)
             weight = jnp.sum(table[8:16] * chosen_ref[...], axis=0, keepdims=True)
             wide = jnp.broadcast_to(member, (16, 128)).astype(BF16)
@@ -320,22 +305,18 @@
                     pick, tokens[dx, dz, :, at : at + size], preferred_element_type=F32
                 ).astype(BF16)
         scale = jnp.concatenate(scales, axis=0)
-        for at, size in chunks(2 * inner, 512):
-            hidden[:, at : at + size] = jnp.dot(
-                packed[...], gate_up[:, at : at + size], preferred_element_type=F32
-            )
-        gate = hidden[:, :inner]
-        up = hidden[:, inner:]
-        act[...] = ((up + 1.0) * gate * jax.nn.sigmoid(1.702 * gate)).astype(BF16)
+        for at, size in chunks(inner, 256):
+            gate = across(packed[...], gate_up[at : at + size])
+            up = across(packed[...], gate_up[inner + at : inner + at + size])
+            act[:, at : at + size] = (
+                (up + 1.0) * gate * jax.nn.sigmoid(1.702 * gate)
+            ).astype(BF16)
         for at, size in chunks(width, 640):
             tile = jnp.dot(act[...], down[:, at : at + size], preferred_element_type=F32)
             tile = (tile * scale).astype(BF16)
             for dz in range(SIDE):
-                parts[dx, dz, :, at : at + size] = lax.dot_general(
-                    picks[dz],
-                    tile[dz * slots : (dz + 1) * slots],
-                    (((0,), (0,)), ((), ())),
-                    preferred_element_type=F32,
+                parts[dx, dz, :, at : at + size] = along(
+                    picks[dz], tile[dz * slots : (dz + 1) * slots]
                 ).astype(BF16)
         return carry
 
@@ -438,11 +419,9 @@
         scratch_shapes=[
             pltpu.VMEM((SIDE, SIDE, rows, width), BF16),
             pltpu.VMEM((SIDE, SIDE, rows, width), BF16),
-            pltpu.VMEM((SIDE, SIDE, 16, rows), F32),
             pltpu.VMEM(gate_up.shape, BF16),
             pltpu.VMEM(down.shape, BF16),
             pltpu.VMEM((SIDE * slots, width), BF16),
-            pltpu.VMEM((SIDE * slots, 2 * inner), F32),
             pltpu.VMEM((SIDE * slots, inner), BF16),
             pltpu.VMEM((SIDE, slots, rows), BF16),
             pltpu.VMEM((2, SIDE, 2, quarter, width), BF16),
@@ -472,6 +451,232 @@
     mine = jnp.sum(jnp.where(jnp.arange(8) == pair, holders, 0))
     chosen = (lax.broadcasted_iota(jnp.int32, (8, ids.shape[0]), 0) == mine).astype(F32)
     return jnp.concatenate([member, weight], axis=0), chosen
+
+
+def project_kernel(
+    tokens_ref,
+    weight_hbm,
+    bias_ref,
+    meta_ref,
+    projected_ref,
+    behind_ref,
+    tables_ref,
+    weight,
+    slices,
+    transit,
+    total,
+    sent,
+    half_in,
+    full_in,
+    behind,
+    tables,
+    local_sem,
+    send_sem,
+    recv_sem,
+):
+    net = Links(send_sem, recv_sem)
+    columns = weight.shape[3]
+    middle = columns // 2
+    rows = projected_ref.shape[0]
+    loads = [
+        pltpu.make_async_copy(
+            weight_hbm.at[:, pl.ds(which * columns, columns)], weight.at[which, 0], local_sem.at[which]
+        )
+        for which in (0, 1)
+    ]
+    for load in loads:
+        load.start()
+    tables[0, 0] = meta_ref[...]
+    place = (net.x, net.z)
+
+    def for_device(which, step, at, size):
+        to = (place[1 - which] + step + SIDE) % SIDE
+        pieces = slice(at, at + size)
+        if which == 0:
+            return lambda: tokens_ref.at[pieces, to]
+        return lambda: tokens_ref.at[to, pieces]
+
+    def kept(which, dq, at, size):
+        lanes = slice(dq * rows, (dq + 1) * rows)
+        pieces = slice(at, at + size)
+        return lambda: slices.at[which, pieces, :, lanes]
+
+    stays = [
+        pltpu.make_async_copy(
+            for_device(which, 0, 0, SIDE)(), kept(which, 0, 0, SIDE)(), local_sem.at[2 + which]
+        )
+        for which in (0, 1)
+    ]
+    for stay in stays:
+        stay.start()
+    net.barrier([(0, 1), (0, -1), (1, 1), (1, -1), (3, 1), (3, -1)])
+    steps = ((0, 1), (1, -1))
+    net.start(("mx", 1), view(tables, 0, 0), view(tables, 0, 3), 0, 1)
+    net.start(("mx", -1), view(tables, 0, 0), view(tables, 0, 1), 0, -1)
+    for which in (0, 1):
+        for side, step in steps:
+            net.start(
+                ("tt", which, step),
+                for_device(which, 2, side * 2, 2),
+                view(transit, which, side),
+                1 - which,
+                step,
+            )
+    for which in (0, 1):
+        for side, step in steps:
+            net.start(
+                ("ta", which, step),
+                for_device(which, step, 0, SIDE),
+                kept(which, (-step) % SIDE, 0, SIDE),
+                1 - which,
+                step,
+            )
+    for which in (0, 1):
+        loads[which].wait()
+        for side, step in steps:
+            net.start(
+                ("wo", which, step),
+                view(weight, which, 0),
+                view(weight, which, (-step) % SIDE),
+                which,
+                step,
+            )
+    net.need(("mx", 1))
+    net.start(("mf", 0), view(tables, 0, 3), view(tables, 0, 2), 0, 1)
+    for which in (0, 1):
+        for side, step in steps:
+            net.need(("tt", which, step))
+            net.start(
+                ("tf", which, step),
+                view(transit, which, side),
+                kept(which, 2, side * 2, 2),
+                1 - which,
+                step,
+            )
+    net.need(("mx", -1), ("mf", 0))
+    net.start(("mz", 1), view(tables, 0), view(tables, 3), 1, 1)
+    net.start(("mz", -1), view(tables, 0), view(tables, 1), 1, -1)
+
+    def multiply(which, dp):
+        piece = (place[which] + dp) % SIDE
+        lhs = slices[which, piece]
+        for at, size in chunks(columns, 640):
+            term = along(lhs, weight[which, dp, :, at : at + size])
+            if dp == 0:
+                total[which, :, at : at + size] = term
+            else:
+                total[which, :, at : at + size] += term
+
+    def pass_on(which, step):
+        net.need(("wo", which, step))
+        part = slice(0, middle) if step == 1 else slice(middle, columns)
+        net.start(
+            ("wf", which, step),
+            lambda: weight.at[which, (-step) % SIDE, :, part],
+            lambda: weight.at[which, 2, :, part],
+            which,
+            step,
+        )
+
+    for which in (0, 1):
+        stays[which].wait()
+        net.need(("ta", which, 1), ("ta", which, -1), ("tf", which, 1), ("tf", which, -1))
+    for which in (0, 1):
+        multiply(which, 0)
+    for step in (1, -1):
+        for which in (0, 1):
+            pass_on(which, step)
+    net.need(("mz", 1), ("mz", -1))
+    net.start(("mg", 0), view(tables, 3), view(tables, 2), 1, 1)
+    for dp in (3, 1):
+        for which in (0, 1):
+            multiply(which, dp)
+    for which in (1, 0):
+        net.need(("wf", which, 1), ("wf", which, -1))
+        multiply(which, 2)
+        sent[which, 2] = total[which, 2 * rows : 3 * rows].astype(BF16)
+        for side, step in steps:
+            part = slice(side * middle, (side + 1) * middle)
+            net.start(
+                ("rh", which, step),
+                view(sent, which, 2, slice(None), part),
+                view(half_in, which, side),
+                1 - which,
+                step,
+            )
+    for which in (1, 0):
+        for side, step in steps:
+            dq = step % SIDE
+            mine = slice(dq * rows, (dq + 1) * rows)
+            part = slice(side * middle, (side + 1) * middle)
+            other = slice((1 - side) * middle, (2 - side) * middle)
+            sent[which, dq, :, other] = total[which, mine, other].astype(BF16)
+            net.need(("rh", which, step))
+            sent[which, dq, :, part] = (
+                total[which, mine, part] + half_in[which, side].astype(F32)
+            ).astype(BF16)
+            net.start(
+                ("rf", which, step),
+                view(sent, which, dq),
+                view(full_in, which, side),
+                1 - which,
+                step,
+            )
+    for which in (1, 0):
+        net.need(("rf", which, 1), ("rf", which, -1))
+        lanes = slice(which * columns, (which + 1) * columns)
+        projected_ref[:, lanes] = (
+            total[which, 0:rows]
+            + full_in[which, 0].astype(F32)
+            + full_in[which, 1].astype(F32)
+            + bias_ref[:, lanes]
+        ).astype(BF16)
+        if which == 1:
+            keys = slice(2 * columns - behind.shape[1], 2 * columns)
+            net.start(
+                ("kv", 0), view(projected_ref, slice(None), keys), view(behind), 3, 1
+            )
+    net.finish()
+    behind_ref[...] = behind[...]
+    tables_ref[...] = tables[...]
+
+
+def project(tokens, weight, bias, meta):
+    depth, rows = tokens.shape[2:]
+    wide = weight.shape[1]
+    columns = wide // 2
+    keys = 2 * KEY_VALUE_HEADS * HEAD_DIM
+    vmem = pl.BlockSpec(memory_space=pltpu.VMEM)
+    return pl.pallas_call(
+        project_kernel,
+        out_shape=(
+            jax.ShapeDtypeStruct((rows, wide), BF16),
+            jax.ShapeDtypeStruct((rows, keys), BF16),
+            jax.ShapeDtypeStruct((SIDE, SIDE, 16, rows), F32),
+        ),
+        in_specs=[vmem, pl.BlockSpec(memory_space=pl.ANY), vmem, vmem],
+        out_specs=(vmem, vmem, vmem),
+        scratch_shapes=[
+            pltpu.VMEM((2, SIDE, depth, columns), BF16),
+            pltpu.VMEM((2, SIDE, depth, SIDE * rows), BF16),
+            pltpu.VMEM((2, 2, 2, depth, rows), BF16),
+            pltpu.VMEM((2, SIDE * rows, columns), F32),
+            pltpu.VMEM((2, SIDE, rows, columns), BF16),
+            pltpu.VMEM((2, 2, rows, columns // 2), BF16),
+            pltpu.VMEM((2, 2, rows, columns), BF16),
+            pltpu.VMEM((rows, keys), BF16),
+            pltpu.VMEM((SIDE, SIDE, 16, rows), F32),
+            pltpu.SemaphoreType.DMA((4,)),
+            pltpu.SemaphoreType.DMA((48,)),
+            pltpu.SemaphoreType.DMA((48,)),
+        ],
+        compiler_params=pltpu.CompilerParams(
+            collective_id=2, has_side_effects=True, vmem_limit_bytes=48 * 1024 * 1024
+        ),
+        cost_estimate=pl.CostEstimate(
+            flops=2_000_000_000, bytes_accessed=4_000_000, transcendentals=0
+        ),
+    )(tokens, weight, bias, meta)
 
 
 def shards(
@@ -496,19 +701,15 @@
     query_group_width = QUERY_HEADS // KEY_VALUE_HEADS
     state = section_input[0]
     normed_in = normed(state, attention_gain[0])
-    projected_rows = (
-        jnp.dot(
-            normed_in,
-            lax.all_gather(query_key_value_weight[0], "expert", axis=0, tiled=True),
-            preferred_element_type=jnp.float32,
-        )
-        + qkv_bias[0]
-    ).astype(jnp.bfloat16)
+    meta, chosen = routing_tables(expert_ids[0], gate_logits[0], placement[0])
+    depth = query_key_value_weight.shape[1]
+    projected_rows, rim_rows, tables = project(
+        normed_in.T.reshape(SIDE, SIDE, depth, count_of_rows), query_key_value_weight[0], qkv_bias, meta
+    )
     query_rows = projected_rows[:, : QUERY_HEADS * HEAD_DIM].reshape(
         count_of_rows, KEY_VALUE_HEADS, query_group_width, HEAD_DIM
     )
     key_value = projected_rows[:, QUERY_HEADS * HEAD_DIM :]
-    rim_rows = from_behind(key_value, "expert", 1)
     rows_in_window = jnp.concatenate([rim_rows, key_value], 0)
     key_row_slice = rows_in_window[:, : KEY_VALUE_HEADS * HEAD_DIM].reshape(
         WINDOW_TOKENS + count_of_rows, KEY_VALUE_HEADS, HEAD_DIM
@@ -542,9 +743,8 @@
         + out_bias[0]
     ).astype(jnp.bfloat16)
     normed_mid = normed(residual, expert_gain[0])
-    meta, chosen = routing_tables(expert_ids[0], gate_logits[0], placement[0])
     moved = experts_and_pass(
-        normed_mid, residual, meta, chosen, gate_up_weight[0, 0], down_weight[0, 0], slots
+        normed_mid, residual, tables, chosen, gate_up_weight[0, 0].T, down_weight[0, 0], slots
     )
     return moved[None]
 

time: 407 us -> 252 us (0.62)
  waiting for transfers between devices: 178 us -> 0 us
  Pallas kernels: 160 us -> 215 us
  local copies, waits for them, and re-layouts: 22.3 us -> 8.51 us
  between operations: 13.7 us -> 0.24 us
  other arithmetic: 5.56 us -> 10.8 us
    all_gather x1 -> x0, waiting for transfers between devices: 178 us -> none  [shards(): lax.all_gather(query_key_value_weight[0], 'expert', axis=0, tiled=True)]
    pallas_call x0 -> x1, Pallas kernels: none -> 50.9 us  [project(): pl.pallas_call(project_kernel, out_shape=(jax.ShapeDtypeStruct((rows, wid...]
    unnamed x30 -> x18, local copies, waits for them, and re-layouts: 18.8 us -> 2.6 us
    dot_general x1 -> x0, matrix products: 11.7 us -> none  [shards(): jnp.dot(normed_in, lax.all_gather(query_key_value_weight[0], 'expert', ax...]
    dot_general x1, matrix products: 4.29 us -> 8.5 us  [shards(): jnp.dot(attended, out_weight[0], preferred_element_type=jnp.float32)]
  transfers between devices with their start and end apart: 2 -> 0, of which waited for: 1 -> 0; matrix products, arithmetic and copies ran while one was open for 4% -> 0% of each run, Pallas kernels for 0% -> 0%
where the time goes in v2:
time: 252 us; the launch traced here: 249 us
  Pallas kernels  215 us (85%)
  matrix products  14.6 us (6%)
  other arithmetic  10.8 us (4%)
  local copies, waits for them, and re-layouts  8.51 us (3%)
    pallas_call x1, Pallas kernels, experts_and_pass(): pl.pallas_call(functools.partial(expert_kernel, slots), out_shape=jax.Sha...  164 us
    pallas_call x1, Pallas kernels, project(): pl.pallas_call(project_kernel, out_shape=(jax.ShapeDtypeStruct((rows, wid...  50.9 us
    dot_general x1, matrix products, shards(): jnp.dot(attended, out_weight[0], preferred_element_type=jnp.float32)  8.5 us

profile of v2, /device:TPU:1, one launch (start us, length us, event | category | flops | bytes accessed | tf_op | source)
XLA Modules:
  0.0 248.8 jit_solution(11818620145905531990)
XLA Ops:
  0.0 0.8 reduce_max.18
  0.8 0.7 fusion.26
  1.5 0.7 divide_bitcast_fusion
  2.2 0.7 convert_reduce_fusion
  2.9 1.5 copy.34
  4.6 0.7 reduce.1
  5.3 0.2 fusion.21
  5.6 1.2 copy.35
  6.7 1.2 reshape.67.tokens_ref
  8.0 50.9 %shard_map.127 = (bf16[128,2560]{1,0:T(8,128)(2,1)S(1)}, bf16[128,512]{1,0:T(8,128)(2,1)S(1)}, f32[4,4,16,128]{3,2,1,0:T(8,128)S(1)}) custom-call(bf16[4,4,180,128]{3,2,1,0:T(8,128)(2,1)S(1)} %reshape.67.tokens_ref, bf16[180,2560]{1,0:T(8,128)(2,1)S(1)} %bitcast.66, f32[1,2560]{1,0:T(1,128)S(1)} %copy-done.1, f32[16,128]{1,0:T(8,128)S(1)} %pad_maximum_fusion.1.meta_ref), custom_call_target="tpu_custom_call" | custom-call | flops 2000000000 | bytes 4000000 | tf_op jit(solution)/shard_map/pallas_call | solution.py:650
  59.0 0.6 copy-done.2
  59.9 0.3 copy.38
  60.2 2.7 %fusion.2 = (f32[4,8,128]{2,1,0:T(8,128)S(1)}, f32[4,256,128,8]{2,1,3,0:T(8,128)}) fusion(pred[128,256]{0,1:T(8,128)(4,1)S(1)} %fusion.24, bf16[256,4,64,1]{0,2,3,1:T(8,128)(2,1)S(1)} %bitcast.70, bf16[128,4,8,64]{0,3,2,1:T(8,128)(2,1)S(1)} %bitcast.67), kind=kOutput, calls=%fused_computation.5 | convolution fusion | flops 137359360 | bytes 4898816 | tf_op jit(solution)/shard_map/ikgd,jkd->kgij/dot_general | solution.py:721
  62.9 0.5 broadcast.83
  63.4 0.6 reduce.7
  64.2 3.2 %fusion.12 = f32[4,8,128]{2,1,0:T(8,128)S(1)} fusion(f32[4,256,128,8]{2,1,3,0:T(8,128)} %get-tuple-element.16, f32[4,8,128]{2,1,0:T(8,128)S(1)} %broadcast_maximum_fusion, pred[128,256]{0,1:T(8,128)(4,1)S(1)} %fusion.24), kind=kLoop, calls=%fused_computation.9 | loop fusion | flops 5238784 | bytes 4259840 | tf_op jit(solution)/shard_map/reduce_sum | solution.py:734
  67.6 3.5 %fusion.20 = bf16[4,64,8,128]{3,1,2,0:T(8,128)(2,1)S(1)} fusion(bf16[256,4,64,1]{0,2,3,1:T(8,128)(2,1)S(1)} %bitcast.71, f32[4,256,128,8]{2,1,3,0:T(8,128)} %get-tuple-element.16, f32[4,8,128]{2,1,0:T(8,128)S(1)} %exponential_add_fusion, f32[4,8,128]{2,1,0:T(8,128)S(1)} %broadcast_maximum_fusion, pred[128,256]{0,1:T(8,128)(4,1)S(1)} %fusion.24), kind=kOutput, calls=%fused_computation.21 | convolution fusion | flops 140771328 | bytes 4915200 | tf_op jit(solution)/shard_map/kgij,jkd->ikgd/dot_general | solution.py:736
  71.1 8.5 %fusion.14 = (f32[128]{0:T(128)S(1)}, bf16[128,2880]{1,0:T(8,128)(2,1)S(1)}) fusion(f32[2880]{0:T(1024)S(1)} %reduce.3, bf16[128,2048]{0,1:T(8,128)(2,1)S(1)} %bitcast.69, bf16[1,2048,2880]{1,2,0:T(8,128)(2,1)} %param.17, bf16[1,128,2880]{2,1,0:T(8,128)(2,1)S(1)} %copy.34), kind=kOutput, calls=%fused_computation.15 | convolution fusion | flops 1512529792 | bytes 13807360 | tf_op jit(solution)/shard_map/dot_general | solution.py:742
  79.7 1.1 fusion.16.normed_ref
  80.8 0.7 fusion.27
  81.5 0.6 compare_convert_fusion
  82.2 0.7 iota.31.chosen_ref
  82.8 163.7 %shard_map.128 = bf16[128,2880]{1,0:T(8,128)(2,1)} custom-call(bf16[128,2880]{1,0:T(8,128)(2,1)} %fusion.16.normed_ref, bf16[128,2880]{1,0:T(8,128)(2,1)} %copy-done.3, f32[4,4,16,128]{3,2,1,0:T(8,128)} %copy-done.2, f32[8,128]{1,0:T(8,128)} %iota.31.chosen_ref, bf16[1440,2880]{1,0:T(8,128)(2,1)} %bitcast.73, bf16[720,2880]{1,0:T(8,128)(2,1)} %bitcast.74), custom_call_target="tpu_custom_call" | custom-call | flops 16000000000 | bytes 16000000 | tf_op jit(solution)/shard_map/pallas_call | solution.py:414
  246.6 2.3 copy.41
  (33 shorter events, 1.0 us)
Async XLA Ops:
  0.0 8.0 %copy-start = (bf16[1,180,2560]{2,1,0:T(8,128)(2,1)S(1)}, bf16[1,180,2560]{2,1,0:T(8,128)(2,1)}, u32[]{:S(2)}) copy-start(bf16[1,180,2560]{2,1,0:T(8,128)(2,1)} %param.15) | copy-start | bytes 2764804
  0.0 8.0 %copy-start.1 = (f32[1,2560]{1,0:T(1,128)S(1)}, f32[1,2560]{1,0:T(1,128)}, u32[]{:S(2)}) copy-start(f32[1,2560]{1,0:T(1,128)} %bias_ref.1) | copy-start | bytes 30724
  58.9 0.7 copy-start.2
  58.9 4.5 %copy-start.6 = (f32[1,32]{1,0:T(1,128)S(1)}, f32[1,32]{1,0:T(1,128)}, u32[]{:S(2)}) copy-start(f32[1,32]{1,0:T(1,128)} %param.19) | copy-start | bytes 388
  67.6 3.5 %copy-start.4 = (f32[1,2880]{1,0:T(1,128)S(1)}, f32[1,2880]{1,0:T(1,128)}, u32[]{:S(2)}) copy-start(f32[1,2880]{1,0:T(1,128)} %param.18) | copy-start | bytes 34564
  71.1 8.5 %copy-start.5 = (f32[1,2880]{1,0:T(1,128)S(1)}, f32[1,2880]{1,0:T(1,128)}, u32[]{:S(2)}) copy-start(f32[1,2880]{1,0:T(1,128)} %param.20) | copy-start | bytes 34564
  71.1 9.7 %copy-start.7 = (s32[1,8]{1,0:T(1,128)S(1)}, s32[1,8]{1,0:T(1,128)}, u32[]{:S(2)}) copy-start(s32[1,8]{1,0:T(1,128)} %param.25) | copy-start | bytes 100
  79.6 3.2 %copy-start.3 = (bf16[128,2880]{1,0:T(8,128)(2,1)}, bf16[128,2880]{1,0:T(8,128)(2,1)S(1)}, u32[]{:S(2)}) copy-start(bf16[128,2880]{1,0:T(8,128)(2,1)S(1)} %get-tuple-element.18.residual_ref) | copy-start | bytes 2211844

commit v3 on v2

--- a/solution.py
+++ b/solution.py
@@ -85,6 +85,16 @@
         for name in self.made:
             self.need(name)
             self.remake(name).wait_send()
+
+
+def of_four(g, values):
+    a, b, c, d = values
+    return (
+        b * (g * (g - 2) * (g - 3)) // 2
+        - c * (g * (g - 1) * (g - 3)) // 2
+        + d * (g * (g - 1) * (g - 2)) // 6
+        - a * ((g - 1) * (g - 2) * (g - 3)) // 6
+    )
 
 
 def add_rows(dst, *parts):
@@ -210,8 +220,14 @@
                     which,
                     step,
                 )
-                on_across(which, dp, 1)
-                on_across(which, dp, -1)
+        for which in (0, 1):
+            on_across(which, 3, 1)
+            on_across(which, 3, -1)
+
+    def other_hops():
+        for which in (0, 1):
+            on_across(which, 1, 1)
+            on_across(which, 1, -1)
 
     def far_hops():
         for half in (1, -1):
@@ -243,8 +259,8 @@
                     step,
                 )
 
-    def arrived(dx):
-        for dz in range(SIDE):
+    def arrived(blocks):
+        for dx, dz in blocks:
             for which in (0, 1):
                 dp, dq = (dx, dz) if which == 0 else (dz, dx)
                 step = {1: -1, 3: 1}
@@ -262,76 +278,30 @@
                 else:
                     net.need(("pq", which, dp, step[dq]))
 
+    groups = (
+        ((0, 0), (1, 0), (3, 0), (0, 1)),
+        ((0, 3), (0, 2), (2, 0), (3, 3)),
+        ((1, 1), (1, 3), (3, 1), (3, 2)),
+        ((2, 3), (1, 2), (2, 1), (2, 2)),
+    )
+
     def stage(at):
         if at == 0:
             first_hops()
-            far_hops()
             second_hops(0)
+            other_hops()
             load_gate_up.wait()
             load_down.wait()
-            arrived(0)
         elif at == 1:
+            far_hops()
+            second_hops(3)
+        elif at == 2:
             second_hops(1)
-            second_hops(3)
-            arrived(1)
-        elif at == 2:
             second_hops(2)
-            arrived(3)
+            back(0)
         else:
-            arrived(2)
-
-    before = lax.broadcasted_iota(jnp.int32, (128, 128), 0)
-    after = lax.broadcasted_iota(jnp.int32, (128, 128), 1)
-    earlier = jnp.where(before < after, 1.0, 0.0).astype(BF16)
-    slot = lax.broadcasted_iota(jnp.int32, (slots, 128), 0).astype(F32)
-
-    def group(g, carry):
-        for at in range(SIDE):
-            pl.when(g == at)(functools.partial(stage, at))
-        dx = g + g // 2 - 2 * (g // 3)
-        scales = []
-        for dz in range(SIDE):
-            table = meta_ref[dz, dx]
-            member = jnp.sum(table[0:8] * chosen_ref[...], axis=0, keepdims=True)
-            weight = jnp.sum(table[8:16] * chosen_ref[...], axis=0, keepdims=True)
-            wide = jnp.broadcast_to(member, (16, 128)).astype(BF16)
-            rank = jnp.dot(wide, earlier, preferred_element_type=F32)[0:1]
-            hit = (slot == rank) & (member > 0.5)
-            pick = jnp.where(hit, 1.0, 0.0).astype(BF16)
-            scales.append(jnp.sum(jnp.where(hit, weight, 0.0), axis=1, keepdims=True))
-            picks[dz] = pick
-            for at, size in chunks(width, 1024):
-                packed[dz * slots : (dz + 1) * slots, at : at + size] = jnp.dot(
-                    pick, tokens[dx, dz, :, at : at + size], preferred_element_type=F32
-                ).astype(BF16)
-        scale = jnp.concatenate(scales, axis=0)
-        for at, size in chunks(inner, 256):
-            gate = across(packed[...], gate_up[at : at + size])
-            up = across(packed[...], gate_up[inner + at : inner + at + size])
-            act[:, at : at + size] = (
-                (up + 1.0) * gate * jax.nn.sigmoid(1.702 * gate)
-            ).astype(BF16)
-        for at, size in chunks(width, 640):
-            tile = jnp.dot(act[...], down[:, at : at + size], preferred_element_type=F32)
-            tile = (tile * scale).astype(BF16)
-            for dz in range(SIDE):
-                parts[dx, dz, :, at : at + size] = along(
-                    picks[dz], tile[dz * slots : (dz + 1) * slots]
-                ).astype(BF16)
-        return carry
-
-    lax.fori_loop(0, SIDE, group, 0)
-
-    for dp in (2, 1, 3, 0):
-        for which in (0, 1):
-            for side, step in ((0, 1), (1, -1)):
-                net.start(
-                    ("rh", which, dp, step),
-                    part(which, dp, 2, at_of(step), quarter),
-                    view(half_in, which, dp, side),
-                    1 - which,
-                    step,
-                )
+            relay(0)
+        arrived(groups[at])
 
     def relay(dp):
         for which in (0, 1):
@@ -347,6 +317,62 @@
                     step,
                 )
 
+    def back(dp):
+        for which in (0, 1):
+            for side, step in ((0, 1), (1, -1)):
+                net.start(
+                    ("rh", which, dp, step),
+                    part(which, dp, 2, at_of(step), quarter),
+                    view(half_in, which, dp, side),
+                    1 - which,
+                    step,
+                )
+
+    before = lax.broadcasted_iota(jnp.int32, (128, 128), 0)
+    after = lax.broadcasted_iota(jnp.int32, (128, 128), 1)
+    earlier = jnp.where(before < after, 1.0, 0.0).astype(BF16)
+    slot = lax.broadcasted_iota(jnp.int32, (slots, 128), 0).astype(F32)
+
+    def group(g, carry):
+        for at in range(SIDE):
+            pl.when(g == at)(functools.partial(stage, at))
+        places = [[of_four(g, [group[k][axis] for group in groups]) for axis in (0, 1)] for k in range(SIDE)]
+        scales = []
+        for k, (dx, dz) in enumerate(places):
+            table = meta_ref[dz, dx]
+            member = jnp.sum(table[0:8] * chosen_ref[...], axis=0, keepdims=True)
+            weight = jnp.sum(table[8:16] * chosen_ref[...], axis=0, keepdims=True)
+            wide = jnp.broadcast_to(member, (16, 128)).astype(BF16)
+            rank = jnp.dot(wide, earlier, preferred_element_type=F32)[0:1]
+            hit = (slot == rank) & (member > 0.5)
+            pick = jnp.where(hit, 1.0, 0.0).astype(BF16)
+            scales.append(jnp.sum(jnp.where(hit, weight, 0.0), axis=1, keepdims=True))
+            picks[k] = pick
+            for at, size in chunks(width, 1024):
+                packed[k * slots : (k + 1) * slots, at : at + size] = jnp.dot(
+                    pick, tokens[dx, dz, :, at : at + size], preferred_element_type=F32
+                ).astype(BF16)
+        scale = jnp.concatenate(scales, axis=0)
+        for at, size in chunks(inner, 256):
+            gate = across(packed[...], gate_up[at : at + size])
+            up = across(packed[...], gate_up[inner + at : inner + at + size])
+            act[:, at : at + size] = (
+                (up + 1.0) * gate * jax.nn.sigmoid(1.702 * gate)
+            ).astype(BF16)
+        for at, size in chunks(width, 640):
+            tile = jnp.dot(act[...], down[:, at : at + size], preferred_element_type=F32)
+            tile = (tile * scale).astype(BF16)
+            for k, (dx, dz) in enumerate(places):
+                parts[dx, dz, :, at : at + size] = along(
+                    picks[k], tile[k * slots : (k + 1) * slots]
+                ).astype(BF16)
+        return carry
+
+    lax.fori_loop(0, SIDE, group, 0)
+
+    for dp in (2, 1, 3):
+        back(dp)
+
     def gather_in(dp):
         for which in (0, 1):
             net.need(("rf", which, dp, 1), ("rf", which, dp, -1))
@@ -363,18 +389,21 @@
                 step,
             )
 
-    def last_full(which):
-        for side, step in ((0, 1), (1, -1)):
+    def last_full(step):
+        side = (1 - step) // 2
+        for which in (0, 1):
             net.need(("lh", which, step))
             there = part(which, step % SIDE, 0, at_of(step), quarter)
             add_rows(there(), there(), half_last.at[which, side])
-            net.start(
-                ("lf", which, step),
-                part(which, step % SIDE, 0, 0, half_rows),
-                view(full_last, which, side),
-                which,
-                step,
-            )
+            for piece in (0, 1):
+                rows = slice(piece * quarter, (piece + 1) * quarter)
+                net.start(
+                    ("lf", which, step, piece),
+                    part(which, step % SIDE, 0, piece * quarter, quarter),
+                    view(full_last, which, side, rows),
+                    which,
+                    step,
+                )
 
     relay(2)
     relay(1)
@@ -383,25 +412,28 @@
     last_half(1)
     relay(3)
     gather_in(1)
-    relay(0)
+    last_full(1)
     gather_in(3)
-    last_full(0)
-    last_full(1)
+    last_full(-1)
     for which in (0, 1):
         net.need(("rf", which, 0, 1), ("rf", which, 0, -1))
-        net.need(("lf", which, 1), ("lf", which, -1))
-        here = part(which, 0, 0, 0, half_rows)
-        rows = slice(which * half_rows, (which + 1) * half_rows)
-        add_rows(
-            here(),
-            here(),
-            full_in.at[which, 0, 0],
-            full_in.at[which, 0, 1],
-            full_last.at[which, 0],
-            full_last.at[which, 1],
-            residual_ref.at[rows],
-        )
-        net.start(("out", which), here, view(out_ref, rows), 2, 1)
+    for piece in (0, 1):
+        for which in (0, 1):
+            net.need(("lf", which, 1, piece), ("lf", which, -1, piece))
+            here = part(which, 0, 0, piece * quarter, quarter)
+            inside = slice(piece * quarter, (piece + 1) * quarter)
+            at = which * half_rows + piece * quarter
+            rows = slice(at, at + quarter)
+            add_rows(
+                here(),
+                here(),
+                full_in.at[which, 0, 0, inside],
+                full_in.at[which, 0, 1, inside],
+                full_last.at[which, 0, inside],
+                full_last.at[which, 1, inside],
+                residual_ref.at[rows],
+            )
+            net.start(("out", which, piece), here, view(out_ref, rows), 2, 1)
     net.finish()
 
 

time: 252 us -> 225 us (0.89); the launches traced: 249 us -> 225 us
  Pallas kernels: 215 us -> 191 us
    pallas_call x1, Pallas kernels: 164 us -> 140 us  [experts_and_pass(): pl.pallas_call(functools.partial(expert_kernel, slots), out_shape=jax.Sha...]
where the time goes in v3:
time: 225 us
  Pallas kernels  191 us (85%)
  matrix products  14.6 us (6%)
  other arithmetic  10.8 us (5%)
  local copies, waits for them, and re-layouts  8.51 us (4%)
    pallas_call x1, Pallas kernels, experts_and_pass(): pl.pallas_call(functools.partial(expert_kernel, slots), out_shape=jax.Sha...  140 us
    pallas_call x1, Pallas kernels, project(): pl.pallas_call(project_kernel, out_shape=(jax.ShapeDtypeStruct((rows, wid...  50.9 us
    dot_general x1, matrix products, shards(): jnp.dot(attended, out_weight[0], preferred_element_type=jnp.float32)  8.5 us

profile of v3, /device:TPU:1, one launch (start us, length us, event | category | flops | bytes accessed | tf_op | source)
XLA Modules:
  0.0 224.8 jit_solution(10969238345489220248)
XLA Ops:
  0.0 0.8 reduce_max.18
  0.8 0.7 fusion.26
  1.5 0.7 divide_bitcast_fusion
  2.2 0.7 convert_reduce_fusion
  2.9 1.5 copy.34
  4.6 0.7 reduce.1
  5.3 0.2 fusion.21
  5.6 1.2 copy.35
  6.7 1.2 reshape.67.tokens_ref
  8.0 50.9 %shard_map.127 = (bf16[128,2560]{1,0:T(8,128)(2,1)S(1)}, bf16[128,512]{1,0:T(8,128)(2,1)S(1)}, f32[4,4,16,128]{3,2,1,0:T(8,128)S(1)}) custom-call(bf16[4,4,180,128]{3,2,1,0:T(8,128)(2,1)S(1)} %reshape.67.tokens_ref, bf16[180,2560]{1,0:T(8,128)(2,1)S(1)} %bitcast.66, f32[1,2560]{1,0:T(1,128)S(1)} %copy-done.1, f32[16,128]{1,0:T(8,128)S(1)} %pad_maximum_fusion.1.meta_ref), custom_call_target="tpu_custom_call" | custom-call | flops 2000000000 | bytes 4000000 | tf_op jit(solution)/shard_map/pallas_call | solution.py:682
  59.0 0.6 copy-done.2
  59.9 0.3 copy.38
  60.2 2.7 %fusion.2 = (f32[4,8,128]{2,1,0:T(8,128)S(1)}, f32[4,256,128,8]{2,1,3,0:T(8,128)}) fusion(pred[128,256]{0,1:T(8,128)(4,1)S(1)} %fusion.24, bf16[256,4,64,1]{0,2,3,1:T(8,128)(2,1)S(1)} %bitcast.70, bf16[128,4,8,64]{0,3,2,1:T(8,128)(2,1)S(1)} %bitcast.67), kind=kOutput, calls=%fused_computation.5 | convolution fusion | flops 137359360 | bytes 4898816 | tf_op jit(solution)/shard_map/ikgd,jkd->kgij/dot_general | solution.py:753
  62.9 0.5 broadcast.83
  63.4 0.6 reduce.7
  64.2 3.2 %fusion.12 = f32[4,8,128]{2,1,0:T(8,128)S(1)} fusion(f32[4,256,128,8]{2,1,3,0:T(8,128)} %get-tuple-element.16, f32[4,8,128]{2,1,0:T(8,128)S(1)} %broadcast_maximum_fusion, pred[128,256]{0,1:T(8,128)(4,1)S(1)} %fusion.24), kind=kLoop, calls=%fused_computation.9 | loop fusion | flops 5238784 | bytes 4259840 | tf_op jit(solution)/shard_map/reduce_sum | solution.py:766
  67.6 3.5 %fusion.20 = bf16[4,64,8,128]{3,1,2,0:T(8,128)(2,1)S(1)} fusion(bf16[256,4,64,1]{0,2,3,1:T(8,128)(2,1)S(1)} %bitcast.71, f32[4,256,128,8]{2,1,3,0:T(8,128)} %get-tuple-element.16, f32[4,8,128]{2,1,0:T(8,128)S(1)} %exponential_add_fusion, f32[4,8,128]{2,1,0:T(8,128)S(1)} %broadcast_maximum_fusion, pred[128,256]{0,1:T(8,128)(4,1)S(1)} %fusion.24), kind=kOutput, calls=%fused_computation.21 | convolution fusion | flops 140771328 | bytes 4915200 | tf_op jit(solution)/shard_map/kgij,jkd->ikgd/dot_general | solution.py:768
  71.1 8.5 %fusion.14 = (f32[128]{0:T(128)S(1)}, bf16[128,2880]{1,0:T(8,128)(2,1)S(1)}) fusion(f32[2880]{0:T(1024)S(1)} %reduce.3, bf16[128,2048]{0,1:T(8,128)(2,1)S(1)} %bitcast.69, bf16[1,2048,2880]{1,2,0:T(8,128)(2,1)} %param.17, bf16[1,128,2880]{2,1,0:T(8,128)(2,1)S(1)} %copy.34), kind=kOutput, calls=%fused_computation.15 | convolution fusion | flops 1512529792 | bytes 13807360 | tf_op jit(solution)/shard_map/dot_general | solution.py:774
  79.7 1.1 fusion.16.normed_ref
  80.8 0.7 fusion.27
  81.5 0.6 compare_convert_fusion
  82.2 0.7 iota.31.chosen_ref
  82.8 139.8 %shard_map.128 = bf16[128,2880]{1,0:T(8,128)(2,1)} custom-call(bf16[128,2880]{1,0:T(8,128)(2,1)} %fusion.16.normed_ref, bf16[128,2880]{1,0:T(8,128)(2,1)} %copy-done.3, f32[4,4,16,128]{3,2,1,0:T(8,128)} %copy-done.2, f32[8,128]{1,0:T(8,128)} %iota.31.chosen_ref, bf16[1440,2880]{1,0:T(8,128)(2,1)} %bitcast.73, bf16[720,2880]{1,0:T(8,128)(2,1)} %bitcast.74), custom_call_target="tpu_custom_call" | custom-call | flops 16000000000 | bytes 16000000 | tf_op jit(solution)/shard_map/pallas_call | solution.py:446
  222.6 2.3 %copy.41 = bf16[1,128,2880]{1,2,0:T(8,128)(2,1)} copy(bf16[1,128,2880]{2,1,0:T(8,128)(2,1)} %bitcast.68) | data formatting | bytes 1474560 | tf_op jit(solution)/shard_map/broadcast_in_dim | solution.py:781
  (33 shorter events, 1.0 us)
Async XLA Ops:
  0.0 8.0 %copy-start = (bf16[1,180,2560]{2,1,0:T(8,128)(2,1)S(1)}, bf16[1,180,2560]{2,1,0:T(8,128)(2,1)}, u32[]{:S(2)}) copy-start(bf16[1,180,2560]{2,1,0:T(8,128)(2,1)} %param.15) | copy-start | bytes 2764804
  0.0 8.0 %copy-start.1 = (f32[1,2560]{1,0:T(1,128)S(1)}, f32[1,2560]{1,0:T(1,128)}, u32[]{:S(2)}) copy-start(f32[1,2560]{1,0:T(1,128)} %bias_ref.1) | copy-start | bytes 30724
  58.9 0.7 copy-start.2
  58.9 4.5 %copy-start.6 = (f32[1,32]{1,0:T(1,128)S(1)}, f32[1,32]{1,0:T(1,128)}, u32[]{:S(2)}) copy-start(f32[1,32]{1,0:T(1,128)} %param.19) | copy-start | bytes 388
  67.6 3.5 %copy-start.4 = (f32[1,2880]{1,0:T(1,128)S(1)}, f32[1,2880]{1,0:T(1,128)}, u32[]{:S(2)}) copy-start(f32[1,2880]{1,0:T(1,128)} %param.18) | copy-start | bytes 34564
  71.1 8.5 %copy-start.5 = (f32[1,2880]{1,0:T(1,128)S(1)}, f32[1,2880]{1,0:T(1,128)}, u32[]{:S(2)}) copy-start(f32[1,2880]{1,0:T(1,128)} %param.20) | copy-start | bytes 34564
  71.1 9.7 %copy-start.7 = (s32[1,8]{1,0:T(1,128)S(1)}, s32[1,8]{1,0:T(1,128)}, u32[]{:S(2)}) copy-start(s32[1,8]{1,0:T(1,128)} %param.25) | copy-start | bytes 100
  79.6 3.2 %copy-start.3 = (bf16[128,2880]{1,0:T(8,128)(2,1)}, bf16[128,2880]{1,0:T(8,128)(2,1)S(1)}, u32[]{:S(2)}) copy-start(bf16[128,2880]{1,0:T(8,128)(2,1)S(1)} %get-tuple-element.18.residual_ref) | copy-start | bytes 2211844

commit v4 on v3

--- a/solution.py
+++ b/solution.py
@@ -10,18 +10,11 @@
 HEAD_DIM = 64
 QUERY_HEADS = 32
 KEY_VALUE_HEADS = 4
-WINDOW_TOKENS = 128
 TOP = 4
 SIDE = 4
 MESH = pl.DeviceIdType.MESH
 F32 = jnp.float32
 BF16 = jnp.bfloat16
-
-
-def normed(vector, gain_row):
-    as_float = vector.astype(jnp.float32)
-    inverse_rms = lax.rsqrt(jnp.mean(as_float * as_float, axis=-1, keepdims=True) + 1e-05)
-    return (as_float * inverse_rms * gain_row).astype(jnp.bfloat16)
 
 
 class Links:
@@ -132,7 +125,7 @@
     normed_ref,
     residual_ref,
     meta_ref,
-    chosen_ref,
+    holders_ref,
     gate_up_hbm,
     down_hbm,
     out_ref,
@@ -333,6 +326,11 @@
     earlier = jnp.where(before < after, 1.0, 0.0).astype(BF16)
     slot = lax.broadcasted_iota(jnp.int32, (slots, 128), 0).astype(F32)
 
+    pair = lax.axis_index("expert") // 2
+    at_pair = lax.broadcasted_iota(jnp.int32, (1, 8), 1) == pair
+    mine = jnp.sum(jnp.where(at_pair, holders_ref[...], 0), axis=1, keepdims=True)
+    chosen = jnp.where(lax.broadcasted_iota(jnp.int32, (8, 128), 0) == mine, 1.0, 0.0)
+
     def group(g, carry):
         for at in range(SIDE):
             pl.when(g == at)(functools.partial(stage, at))
@@ -340,8 +338,8 @@
         scales = []
         for k, (dx, dz) in enumerate(places):
             table = meta_ref[dz, dx]
-            member = jnp.sum(table[0:8] * chosen_ref[...], axis=0, keepdims=True)
-            weight = jnp.sum(table[8:16] * chosen_ref[...], axis=0, keepdims=True)
+            member = jnp.sum(table[0:8] * chosen, axis=0, keepdims=True)
+            weight = jnp.sum(table[8:16] * chosen, axis=0, keepdims=True)
             wide = jnp.broadcast_to(member, (16, 128)).astype(BF16)
             rank = jnp.dot(wide, earlier, preferred_element_type=F32)[0:1]
             hit = (slot == rank) & (member > 0.5)
@@ -437,7 +435,7 @@
     net.finish()
 
 
-def experts_and_pass(normed_mid, residual, meta, chosen, gate_up, down, slots):
+def experts_and_pass(normed_mid, residual, meta, holders, gate_up, down, slots):
     rows, width = normed_mid.shape
     inner = down.shape[0]
     anywhere = pl.BlockSpec(memory_space=pl.ANY)
@@ -470,29 +468,90 @@
         cost_estimate=pl.CostEstimate(
             flops=16_000_000_000, bytes_accessed=16_000_000, transcendentals=1_000_000
         ),
-    )(normed_mid, residual, meta, chosen, gate_up, down)
-
-
-def routing_tables(ids, logits, holders):
-    kinds = lax.broadcasted_iota(jnp.int32, (8, ids.shape[0], TOP), 0)
-    equal = (ids[None] == kinds).astype(F32)
-    weights = jax.nn.softmax(logits, axis=-1)
-    member = jnp.sum(equal, axis=-1)
-    weight = jnp.sum(equal * weights[None], axis=-1)
-    pair = lax.axis_index("expert") // 2
-    mine = jnp.sum(jnp.where(jnp.arange(8) == pair, holders, 0))
-    chosen = (lax.broadcasted_iota(jnp.int32, (8, ids.shape[0]), 0) == mine).astype(F32)
-    return jnp.concatenate([member, weight], axis=0), chosen
+    )(normed_mid, residual, meta, holders, gate_up, down)
+
+
+def routing_tables(ids, logits):
+    kinds = lax.broadcasted_iota(jnp.int32, (8, ids.shape[1]), 0)
+    grown = jnp.exp(logits - jnp.max(logits, axis=0, keepdims=True))
+    weights = grown / jnp.sum(grown, axis=0, keepdims=True)
+    member, weight = jnp.zeros(kinds.shape, F32), jnp.zeros(kinds.shape, F32)
+    for k in range(TOP):
+        equal = kinds == ids[k : k + 1]
+        member = member + jnp.where(equal, 1.0, 0.0)
+        weight = weight + jnp.where(equal, weights[k : k + 1], 0.0)
+    return member, weight
+
+
+def attend(projected, behind, sinks_ref, attended, first):
+    rows = projected.shape[0]
+    pair = 2 * HEAD_DIM
+    group = QUERY_HEADS // KEY_VALUE_HEADS
+    row = lax.broadcasted_iota(jnp.int32, (rows, rows), 0)
+    lane = lax.broadcasted_iota(jnp.int32, (rows, rows), 1)
+    low = lax.broadcasted_iota(jnp.int32, (rows, pair), 1) < HEAD_DIM
+    older = row > lane
+    scale = jnp.where(first, 0.0, 0.125)
+    offset = jnp.where(first, -1e30, 0.0)
+    keys_at = QUERY_HEADS * HEAD_DIM
+    values_at = keys_at + KEY_VALUE_HEADS * HEAD_DIM
+    for g in range(KEY_VALUE_HEADS):
+        tile = g // 2 * pair
+        stacked = []
+        own = projected[:, keys_at + tile : keys_at + tile + pair].astype(F32)
+        rim = behind[:, tile : tile + pair].astype(F32)
+        for side in (0, 1):
+            for keys in (rim, own):
+                placed = keys if g % 2 == side else pltpu.roll(keys, HEAD_DIM, 1)
+                stacked.append(jnp.where(low if side == 0 else ~low, placed, 0.0).astype(BF16))
+        keys = jnp.concatenate(stacked, axis=0)
+        at = values_at + tile
+        values = jnp.concatenate(
+            [
+                behind[:, KEY_VALUE_HEADS * HEAD_DIM + tile : KEY_VALUE_HEADS * HEAD_DIM + tile + pair],
+                projected[:, at : at + pair],
+            ],
+            axis=0,
+        ).astype(F32)
+        values = values.T[g % 2 * HEAD_DIM : (g % 2 + 1) * HEAD_DIM].astype(BF16)
+        for head in range(g * group, (g + 1) * group, 2):
+            scores = across(keys, projected[:, head * HEAD_DIM : head * HEAD_DIM + pair])
+            for side in (0, 1):
+                past = scores[2 * side * rows : (2 * side + 1) * rows]
+                here = scores[(2 * side + 1) * rows : (2 * side + 2) * rows]
+                merged = jnp.where(older, past * scale + offset, here * 0.125)
+                sink = sinks_ref[0, head + side]
+                peak = jnp.maximum(jnp.max(merged, axis=0, keepdims=True), sink)
+                numer = jnp.exp(merged - peak)
+                denominator = jnp.sum(numer, axis=0, keepdims=True) + jnp.exp(sink - peak)
+                share = numer * (1.0 / denominator)
+                both = jnp.concatenate(
+                    [jnp.where(older, share, 0.0), jnp.where(older, 0.0, share)], axis=0
+                ).astype(BF16)
+                attended[(head + side) * HEAD_DIM : (head + side + 1) * HEAD_DIM] = jnp.dot(
+                    values, both, preferred_element_type=F32
+                ).astype(BF16)
 
 
 def project_kernel(
-    tokens_ref,
+    pieces_ref,
+    gains_ref,
+    state_ref,
     weight_hbm,
     bias_ref,
-    meta_ref,
+    ids_ref,
+    logits_ref,
+    sinks_ref,
+    out_weight_hbm,
+    out_bias_ref,
+    mid_gain_ref,
+    normed_ref,
+    residual_ref,
+    tables_ref,
     projected_ref,
-    behind_ref,
-    tables_ref,
+    tokens_ref,
+    out_weight,
+    attended,
     weight,
     slices,
     transit,
@@ -518,8 +577,13 @@
     ]
     for load in loads:
         load.start()
-    tables[0, 0] = meta_ref[...]
+    load_out = pltpu.make_async_copy(out_weight_hbm, out_weight, local_sem.at[4])
+    load_out.start()
+    member, gate_weight = routing_tables(ids_ref[...], logits_ref[...])
+    tables[0, 0, 0:8] = member
+    tables[0, 0, 8:16] = gate_weight
     place = (net.x, net.z)
+    features = state_ref.shape[0]
 
     def for_device(which, step, at, size):
         to = (place[1 - which] + step + SIDE) % SIDE
@@ -533,6 +597,30 @@
         pieces = slice(at, at + size)
         return lambda: slices.at[which, pieces, :, lanes]
 
+    net.barrier([(0, 1), (0, -1), (1, 1), (1, -1), (3, 1), (3, -1)])
+    steps = ((0, 1), (1, -1))
+    net.start(("mx", 1), view(tables, 0, 0), view(tables, 0, 3), 0, 1)
+    net.start(("mx", -1), view(tables, 0, 0), view(tables, 0, 1), 0, -1)
+    for which in (0, 1):
+        loads[which].wait()
+        for side, step in steps:
+            net.start(
+                ("wo", which, step),
+                view(weight, which, 0),
+                view(weight, which, (-step) % SIDE),
+                which,
+                step,
+            )
+    squares = jnp.zeros(pieces_ref.shape[2:], F32)
+    for a in range(SIDE):
+        for b in range(SIDE):
+            piece = pieces_ref[a, b].astype(F32)
+            squares = squares + piece * piece
+    inverse = lax.rsqrt(jnp.sum(squares, axis=0, keepdims=True) / features + 1e-05)
+    for a in range(SIDE):
+        for b in range(SIDE):
+            piece = pieces_ref[a, b].astype(F32)
+            tokens_ref[a, b] = (piece * inverse * gains_ref[a, b]).astype(BF16)
     stays = [
         pltpu.make_async_copy(
             for_device(which, 0, 0, SIDE)(), kept(which, 0, 0, SIDE)(), local_sem.at[2 + which]
@@ -541,10 +629,6 @@
     ]
     for stay in stays:
         stay.start()
-    net.barrier([(0, 1), (0, -1), (1, 1), (1, -1), (3, 1), (3, -1)])
-    steps = ((0, 1), (1, -1))
-    net.start(("mx", 1), view(tables, 0, 0), view(tables, 0, 3), 0, 1)
-    net.start(("mx", -1), view(tables, 0, 0), view(tables, 0, 1), 0, -1)
     for which in (0, 1):
         for side, step in steps:
             net.start(
@@ -561,16 +645,6 @@
                 for_device(which, step, 0, SIDE),
                 kept(which, (-step) % SIDE, 0, SIDE),
                 1 - which,
-                step,
-            )
-    for which in (0, 1):
-        loads[which].wait()
-        for side, step in steps:
-            net.start(
-                ("wo", which, step),
-                view(weight, which, 0),
-                view(weight, which, (-step) % SIDE),
-                which,
                 step,
             )
     net.need(("mx", 1))
@@ -669,26 +743,59 @@
                 ("kv", 0), view(projected_ref, slice(None), keys), view(behind), 3, 1
             )
     net.finish()
-    behind_ref[...] = behind[...]
     tables_ref[...] = tables[...]
-
-
-def project(tokens, weight, bias, meta):
-    depth, rows = tokens.shape[2:]
+    attend(projected_ref, behind, sinks_ref, attended, net.x * SIDE + net.z == 0)
+    load_out.wait()
+    squares = jnp.zeros((rows, 1), F32)
+    for at, size in chunks(features, 640):
+        lanes = slice(at, at + size)
+        mixed = jnp.dot(out_weight[lanes], attended[...], preferred_element_type=F32)
+        mixed = mixed + state_ref[lanes].astype(F32)
+        kept_sum = (mixed.T + out_bias_ref[:, lanes]).astype(BF16)
+        residual_ref[:, lanes] = kept_sum
+        wide = kept_sum.astype(F32)
+        squares = squares + jnp.sum(wide * wide, axis=1, keepdims=True)
+    inverse = lax.rsqrt(squares / features + 1e-05)
+    for at, size in chunks(features, 640):
+        lanes = slice(at, at + size)
+        wide = residual_ref[:, lanes].astype(F32)
+        normed_ref[:, lanes] = (wide * inverse * mid_gain_ref[:, lanes]).astype(BF16)
+
+
+def attention_part(pieces, gains, state, weight, bias, ids, logits, sinks, out_weight, out_bias, mid_gain):
+    features, rows = state.shape
+    depth = pieces.shape[2]
     wide = weight.shape[1]
     columns = wide // 2
     keys = 2 * KEY_VALUE_HEADS * HEAD_DIM
+    anywhere = pl.BlockSpec(memory_space=pl.ANY)
     vmem = pl.BlockSpec(memory_space=pltpu.VMEM)
     return pl.pallas_call(
         project_kernel,
         out_shape=(
-            jax.ShapeDtypeStruct((rows, wide), BF16),
-            jax.ShapeDtypeStruct((rows, keys), BF16),
+            jax.ShapeDtypeStruct((rows, features), BF16),
+            jax.ShapeDtypeStruct((rows, features), BF16),
             jax.ShapeDtypeStruct((SIDE, SIDE, 16, rows), F32),
         ),
-        in_specs=[vmem, pl.BlockSpec(memory_space=pl.ANY), vmem, vmem],
+        in_specs=[
+            vmem,
+            vmem,
+            vmem,
+            anywhere,
+            vmem,
+            vmem,
+            vmem,
+            pl.BlockSpec(memory_space=pltpu.SMEM),
+            anywhere,
+            vmem,
+            vmem,
+        ],
         out_specs=(vmem, vmem, vmem),
         scratch_shapes=[
+            pltpu.VMEM((rows, wide), BF16),
+            pltpu.VMEM(pieces.shape, BF16),
+            pltpu.VMEM(out_weight.shape, BF16),
+            pltpu.VMEM((QUERY_HEADS * HEAD_DIM, rows), BF16),
             pltpu.VMEM((2, SIDE, depth, columns), BF16),
             pltpu.VMEM((2, SIDE, depth, SIDE * rows), BF16),
             pltpu.VMEM((2, 2, 2, depth, rows), BF16),
@@ -698,17 +805,17 @@
             pltpu.VMEM((2, 2, rows, columns), BF16),
             pltpu.VMEM((rows, keys), BF16),
             pltpu.VMEM((SIDE, SIDE, 16, rows), F32),
-            pltpu.SemaphoreType.DMA((4,)),
+            pltpu.SemaphoreType.DMA((5,)),
             pltpu.SemaphoreType.DMA((48,)),
             pltpu.SemaphoreType.DMA((48,)),
         ],
         compiler_params=pltpu.CompilerParams(
-            collective_id=2, has_side_effects=True, vmem_limit_bytes=48 * 1024 * 1024
+            collective_id=2, has_side_effects=True, vmem_limit_bytes=56 * 1024 * 1024
         ),
         cost_estimate=pl.CostEstimate(
             flops=2_000_000_000, bytes_accessed=4_000_000, transcendentals=0
         ),
-    )(tokens, weight, bias, meta)
+    )(pieces, gains, state, weight, bias, ids, logits, sinks, out_weight, out_bias, mid_gain)
 
 
 def shards(
@@ -726,57 +833,27 @@
     gate_logits,
     placement,
 ):
-    count_of_rows = section_input.shape[1]
-    experts_count = placement.shape[1]
-    slots = 2 * min(count_of_rows // 2, count_of_rows * TOP * 5 // (8 * experts_count))
-    offset = lax.axis_index("expert") * count_of_rows
-    query_group_width = QUERY_HEADS // KEY_VALUE_HEADS
-    state = section_input[0]
-    normed_in = normed(state, attention_gain[0])
-    meta, chosen = routing_tables(expert_ids[0], gate_logits[0], placement[0])
+    rows, features = section_input.shape[1:]
+    experts = placement.shape[1]
+    slots = 2 * min(rows // 2, rows * TOP * 5 // (8 * experts))
     depth = query_key_value_weight.shape[1]
-    projected_rows, rim_rows, tables = project(
-        normed_in.T.reshape(SIDE, SIDE, depth, count_of_rows), query_key_value_weight[0], qkv_bias, meta
+    state = section_input[0].T
+    apart = (SIDE, SIDE, depth, rows)
+    normed_mid, residual, tables = attention_part(
+        state.reshape(apart),
+        jnp.broadcast_to(attention_gain[0].reshape(apart[:3])[..., None], apart),
+        state,
+        query_key_value_weight[0],
+        qkv_bias,
+        expert_ids[0].T,
+        gate_logits[0].T,
+        attention_sink_logits,
+        out_weight[0].T,
+        out_bias,
+        expert_gain,
     )
-    query_rows = projected_rows[:, : QUERY_HEADS * HEAD_DIM].reshape(
-        count_of_rows, KEY_VALUE_HEADS, query_group_width, HEAD_DIM
-    )
-    key_value = projected_rows[:, QUERY_HEADS * HEAD_DIM :]
-    rows_in_window = jnp.concatenate([rim_rows, key_value], 0)
-    key_row_slice = rows_in_window[:, : KEY_VALUE_HEADS * HEAD_DIM].reshape(
-        WINDOW_TOKENS + count_of_rows, KEY_VALUE_HEADS, HEAD_DIM
-    )
-    value_row_slice = rows_in_window[:, KEY_VALUE_HEADS * HEAD_DIM :].reshape(
-        WINDOW_TOKENS + count_of_rows, KEY_VALUE_HEADS, HEAD_DIM
-    )
-    scores = (
-        jnp.einsum("ikgd,jkd->kgij", query_rows, key_row_slice, preferred_element_type=jnp.float32)
-        * 0.125
-    )
-    query_pos = offset + jnp.arange(count_of_rows, dtype=jnp.int32)
-    key_pos = offset - WINDOW_TOKENS + jnp.arange(WINDOW_TOKENS + count_of_rows, dtype=jnp.int32)
-    distance = query_pos[:, None] - key_pos[None, :]
-    inside = (distance >= 0) & (distance < WINDOW_TOKENS) & (key_pos >= 0)[None, :]
-    head_sink_logit = attention_sink_logits[0].reshape(KEY_VALUE_HEADS, query_group_width)[
-        :, :, None
-    ]
-    masked = jnp.where(inside, scores, -1e30)
-    peak = jnp.maximum(jnp.max(masked, axis=-1), head_sink_logit)
-    numer = jnp.where(inside, jnp.exp(masked - peak[..., None]), 0.0)
-    denominator = jnp.sum(numer, axis=-1) + jnp.exp(head_sink_logit - peak)
-    attention = (numer / denominator[..., None]).astype(jnp.bfloat16)
-    mixed = jnp.einsum(
-        "kgij,jkd->ikgd", attention, value_row_slice, preferred_element_type=jnp.float32
-    )
-    attended = mixed.astype(jnp.bfloat16).reshape(count_of_rows, QUERY_HEADS * HEAD_DIM)
-    residual = (
-        state.astype(jnp.float32)
-        + jnp.dot(attended, out_weight[0], preferred_element_type=jnp.float32)
-        + out_bias[0]
-    ).astype(jnp.bfloat16)
-    normed_mid = normed(residual, expert_gain[0])
     moved = experts_and_pass(
-        normed_mid, residual, tables, chosen, gate_up_weight[0, 0].T, down_weight[0, 0], slots
+        normed_mid, residual, tables, placement, gate_up_weight[0, 0].T, down_weight[0, 0], slots
     )
     return moved[None]
 

time: 225 us -> 209 us (0.929)
  matrix products: 14.6 us -> 0 us
  Pallas kernels: 191 us -> 202 us
  other arithmetic: 10.8 us -> 0.74 us
  local copies, waits for them, and re-layouts: 8.51 us -> 6.01 us
    dot_general x3 -> x0, matrix products: 14.6 us -> none  [the longest x1 8.5 us: shards(): jnp.dot(attended, out_weight[0], preferred_element_type=jnp.float32)]
    pallas_call x1, Pallas kernels: 50.9 us -> 61.8 us  [attention_part(): pl.pallas_call(project_kernel, out_shape=(jax.ShapeDtypeStruct((rows, fea...]
    reduce_sum x5 -> x0, other arithmetic: 5.55 us -> none  [the longest x1 3.23 us: shards(): denominator = jnp.sum(numer, axis=-1) + jnp.exp(head_sink_logit - peak)]
    unnamed x18 -> x0, local copies, waits for them, and re-layouts: 2.6 us -> none
where the time goes in v4:
time: 209 us; the launch traced here: 208 us
  Pallas kernels  202 us (97%)
  local copies, waits for them, and re-layouts  6.01 us (3%)
    pallas_call x1, Pallas kernels, experts_and_pass(): pl.pallas_call(functools.partial(expert_kernel, slots), out_shape=jax.Sha...  140 us
    pallas_call x1, Pallas kernels, attention_part(): pl.pallas_call(project_kernel, out_shape=(jax.ShapeDtypeStruct((rows, fea...  61.8 us

profile of v4, /device:TPU:1, one launch (start us, length us, event | category | flops | bytes accessed | tf_op | source)
XLA Modules:
  0.0 208.4 jit_solution(3267209294043906435)
XLA Ops:
  0.0 0.7 reduce
  0.7 0.1 broadcast_in_dim.10
  0.8 2.0 reshape.4.pieces_ref
  2.9 1.6 broadcast_in_dim.11.gains_ref
  4.5 61.8 %shard_map.127 = (bf16[128,2880]{1,0:T(8,128)(2,1)}, bf16[128,2880]{1,0:T(8,128)(2,1)}, f32[4,4,16,128]{3,2,1,0:T(8,128)}) custom-call(bf16[4,4,180,128]{3,2,1,0:T(8,128)(2,1)} %reshape.4.pieces_ref, f32[4,4,180,128]{3,2,1,0:T(8,128)} %broadcast_in_dim.11.gains_ref, bf16[2880,128]{1,0:T(8,128)(2,1)} %bitcast.20, bf16[180,2560]{1,0:T(8,128)(2,1)} %bitcast.21, ...), custom_call_target="tpu_custom_call" | custom-call | flops 2000000000 | bytes 4000000 | tf_op jit(solution)/shard_map/pallas_call | solution.py:773
  66.3 139.8 %shard_map.128 = bf16[128,2880]{1,0:T(8,128)(2,1)} custom-call(bf16[128,2880]{1,0:T(8,128)(2,1)} %get-tuple-element.8.normed_ref, bf16[128,2880]{1,0:T(8,128)(2,1)} %get-tuple-element.9.residual_ref, f32[4,4,16,128]{3,2,1,0:T(8,128)} %get-tuple-element.10.meta_ref, s32[1,8]{1,0:T(1,128)} %holders_ref.1, bf16[1440,2880]{1,0:T(8,128)(2,1)} %bitcast.25, ...), custom_call_target="tpu_custom_call" | custom-call | flops 16000000000 | bytes 16000000 | tf_op jit(solution)/shard_map/pallas_call | solution.py:444
  206.1 2.3 %copy.15 = bf16[1,128,2880]{1,2,0:T(8,128)(2,1)} copy(bf16[1,128,2880]{2,1,0:T(8,128)(2,1)} %bitcast.22) | data formatting | bytes 1474560 | tf_op jit(solution)/shard_map/broadcast_in_dim | solution.py:858

commit v5 on v4

--- a/solution.py
+++ b/solution.py
@@ -44,6 +44,7 @@
         pl.semaphore_wait(sem, len(partners))
 
     def start(self, name, src, dst, axis, step):
+        assert name not in self.made
         key = self.keys.setdefault(name, len(self.keys))
         copy = pltpu.make_async_remote_copy(
             src_ref=src(),
@@ -534,9 +535,8 @@
 
 
 def project_kernel(
-    pieces_ref,
-    gains_ref,
     state_ref,
+    gain_ref,
     weight_hbm,
     bias_ref,
     ids_ref,
@@ -549,6 +549,7 @@
     residual_ref,
     tables_ref,
     projected_ref,
+    scaled,
     tokens_ref,
     out_weight,
     attended,
@@ -566,16 +567,23 @@
     recv_sem,
 ):
     net = Links(send_sem, recv_sem)
-    columns = weight.shape[3]
-    middle = columns // 2
-    rows = projected_ref.shape[0]
-    loads = [
-        pltpu.make_async_copy(
-            weight_hbm.at[:, pl.ds(which * columns, columns)], weight.at[which, 0], local_sem.at[which]
+    columns = weight.shape[4]
+    rows = normed_ref.shape[0]
+    cuts = (384, 256)
+
+    def column_at(which, chunk):
+        return columns * (chunk if which == 0 else 3 - chunk)
+
+    loads = {
+        (which, chunk): pltpu.make_async_copy(
+            weight_hbm.at[:, pl.ds(column_at(which, chunk), columns)],
+            weight.at[which, chunk, 0],
+            local_sem.at[5 + 2 * which + chunk],
         )
+        for chunk in (0, 1)
         for which in (0, 1)
-    ]
-    for load in loads:
+    }
+    for load in loads.values():
         load.start()
     load_out = pltpu.make_async_copy(out_weight_hbm, out_weight, local_sem.at[4])
     load_out.start()
@@ -601,26 +609,33 @@
     steps = ((0, 1), (1, -1))
     net.start(("mx", 1), view(tables, 0, 0), view(tables, 0, 3), 0, 1)
     net.start(("mx", -1), view(tables, 0, 0), view(tables, 0, 1), 0, -1)
-    for which in (0, 1):
-        loads[which].wait()
+
+    def offer(which, chunk):
+        loads[which, chunk].wait()
         for side, step in steps:
             net.start(
-                ("wo", which, step),
-                view(weight, which, 0),
-                view(weight, which, (-step) % SIDE),
+                ("wo", which, chunk, step),
+                view(weight, which, chunk, 0),
+                view(weight, which, chunk, (-step) % SIDE),
                 which,
                 step,
             )
-    squares = jnp.zeros(pieces_ref.shape[2:], F32)
+
+    for which in (0, 1):
+        offer(which, 0)
+    squares = jnp.zeros((1, rows), F32)
+    for at, size in chunks(features, 640):
+        part = state_ref[at : at + size].astype(F32)
+        squares = squares + jnp.sum(part * part, axis=0, keepdims=True)
+    inverse = lax.rsqrt(squares / features + 1e-05)
+    for at, size in chunks(features, 640):
+        gain = jnp.broadcast_to(gain_ref[:, at : at + size], (rows, size)).T
+        scaled[at : at + size] = state_ref[at : at + size].astype(F32) * inverse * gain
+    depth = tokens_ref.shape[2]
     for a in range(SIDE):
         for b in range(SIDE):
-            piece = pieces_ref[a, b].astype(F32)
-            squares = squares + piece * piece
-    inverse = lax.rsqrt(jnp.sum(squares, axis=0, keepdims=True) / features + 1e-05)
-    for a in range(SIDE):
-        for b in range(SIDE):
-            piece = pieces_ref[a, b].astype(F32)
-            tokens_ref[a, b] = (piece * inverse * gains_ref[a, b]).astype(BF16)
+            at = (a * SIDE + b) * depth
+            tokens_ref[a, b] = scaled[at : at + depth].astype(BF16)
     stays = [
         pltpu.make_async_copy(
             for_device(which, 0, 0, SIDE)(), kept(which, 0, 0, SIDE)(), local_sem.at[2 + which]
@@ -647,8 +662,76 @@
                 1 - which,
                 step,
             )
-    net.need(("mx", 1))
-    net.start(("mf", 0), view(tables, 0, 3), view(tables, 0, 2), 0, 1)
+    def pass_on(which, chunk, step):
+        net.need(("wo", which, chunk, step))
+        part = slice(0, cuts[chunk]) if step == 1 else slice(cuts[chunk], columns)
+        every = slice(None)
+        net.start(
+            ("wf", which, chunk, step),
+            view(weight, which, chunk, (-step) % SIDE, every, part),
+            view(weight, which, chunk, 2, every, part),
+            which,
+            step,
+        )
+
+    def multiply(which, chunk, dp):
+        piece = (place[which] + dp) % SIDE
+        term = along(slices[which, piece], weight[which, chunk, dp])
+        if dp == 0:
+            total[which, chunk] = term
+        else:
+            total[which, chunk] += term
+
+    def half_of(side):
+        return slice(side * rows // 2, (side + 1) * rows // 2)
+
+    def sums_out(which, chunk):
+        net.need(("wf", which, chunk, 1), ("wf", which, chunk, -1))
+        multiply(which, chunk, 2)
+        sent[which, chunk, 2] = total[which, chunk, 2 * rows : 3 * rows].astype(BF16)
+        for side, step in steps:
+            net.start(
+                ("rh", which, chunk, step),
+                view(sent, which, chunk, 2, half_of(side)),
+                view(half_in, which, chunk, side),
+                1 - which,
+                step,
+            )
+
+    def sums_on(which, chunk):
+        for side, step in steps:
+            dq = step % SIDE
+            other = half_of(1 - side)
+            sent[which, chunk, dq, other] = total[
+                which, chunk, dq * rows + other.start : dq * rows + other.stop
+            ].astype(BF16)
+            net.need(("rh", which, chunk, step))
+            part = half_of(side)
+            sent[which, chunk, dq, part] = (
+                total[which, chunk, dq * rows + part.start : dq * rows + part.stop]
+                + half_in[which, chunk, side].astype(F32)
+            ).astype(BF16)
+            net.start(
+                ("rf", which, chunk, step),
+                view(sent, which, chunk, dq),
+                view(full_in, which, chunk, side),
+                1 - which,
+                step,
+            )
+
+    def sums_in(which, chunk):
+        net.need(("rf", which, chunk, 1), ("rf", which, chunk, -1))
+        lanes = slice(column_at(which, chunk), column_at(which, chunk) + columns)
+        projected_ref[:, lanes] = (
+            total[which, chunk, 0:rows]
+            + full_in[which, chunk, 0].astype(F32)
+            + full_in[which, chunk, 1].astype(F32)
+            + bias_ref[:, lanes]
+        ).astype(BF16)
+
+    for step in (1, -1):
+        for which in (0, 1):
+            pass_on(which, 0, step)
     for which in (0, 1):
         for side, step in steps:
             net.need(("tt", which, step))
@@ -659,89 +742,41 @@
                 1 - which,
                 step,
             )
+    for which in (0, 1):
+        offer(which, 1)
+    net.need(("mx", 1))
+    net.start(("mf", 0), view(tables, 0, 3), view(tables, 0, 2), 0, 1)
+    for which in (0, 1):
+        stays[which].wait()
+        net.need(("ta", which, 1), ("ta", which, -1), ("tf", which, 1), ("tf", which, -1))
+    for which in (1, 0):
+        for dp in (0, 3, 1):
+            multiply(which, 0, dp)
+    for which in (1, 0):
+        sums_out(which, 0)
+    for step in (1, -1):
+        for which in (0, 1):
+            pass_on(which, 1, step)
     net.need(("mx", -1), ("mf", 0))
     net.start(("mz", 1), view(tables, 0), view(tables, 3), 1, 1)
     net.start(("mz", -1), view(tables, 0), view(tables, 1), 1, -1)
-
-    def multiply(which, dp):
-        piece = (place[which] + dp) % SIDE
-        lhs = slices[which, piece]
-        for at, size in chunks(columns, 640):
-            term = along(lhs, weight[which, dp, :, at : at + size])
-            if dp == 0:
-                total[which, :, at : at + size] = term
-            else:
-                total[which, :, at : at + size] += term
-
-    def pass_on(which, step):
-        net.need(("wo", which, step))
-        part = slice(0, middle) if step == 1 else slice(middle, columns)
-        net.start(
-            ("wf", which, step),
-            lambda: weight.at[which, (-step) % SIDE, :, part],
-            lambda: weight.at[which, 2, :, part],
-            which,
-            step,
-        )
-
-    for which in (0, 1):
-        stays[which].wait()
-        net.need(("ta", which, 1), ("ta", which, -1), ("tf", which, 1), ("tf", which, -1))
-    for which in (0, 1):
-        multiply(which, 0)
-    for step in (1, -1):
-        for which in (0, 1):
-            pass_on(which, step)
+    for which in (1, 0):
+        sums_on(which, 0)
+    for which in (1, 0):
+        for dp in (0, 3, 1):
+            multiply(which, 1, dp)
+    for which in (1, 0):
+        sums_out(which, 1)
     net.need(("mz", 1), ("mz", -1))
     net.start(("mg", 0), view(tables, 3), view(tables, 2), 1, 1)
-    for dp in (3, 1):
-        for which in (0, 1):
-            multiply(which, dp)
+    sums_in(1, 0)
+    keys = slice(4 * columns - behind.shape[1], 4 * columns)
+    net.start(("kv", 0), view(projected_ref, slice(None), keys), view(behind), 3, 1)
     for which in (1, 0):
-        net.need(("wf", which, 1), ("wf", which, -1))
-        multiply(which, 2)
-        sent[which, 2] = total[which, 2 * rows : 3 * rows].astype(BF16)
-        for side, step in steps:
-            part = slice(side * middle, (side + 1) * middle)
-            net.start(
-                ("rh", which, step),
-                view(sent, which, 2, slice(None), part),
-                view(half_in, which, side),
-                1 - which,
-                step,
-            )
+        sums_on(which, 1)
+    sums_in(0, 0)
     for which in (1, 0):
-        for side, step in steps:
-            dq = step % SIDE
-            mine = slice(dq * rows, (dq + 1) * rows)
-            part = slice(side * middle, (side + 1) * middle)
-            other = slice((1 - side) * middle, (2 - side) * middle)
-            sent[which, dq, :, other] = total[which, mine, other].astype(BF16)
-            net.need(("rh", which, step))
-            sent[which, dq, :, part] = (
-                total[which, mine, part] + half_in[which, side].astype(F32)
-            ).astype(BF16)
-            net.start(
-                ("rf", which, step),
-                view(sent, which, dq),
-                view(full_in, which, side),
-                1 - which,
-                step,
-            )
-    for which in (1, 0):
-        net.need(("rf", which, 1), ("rf", which, -1))
-        lanes = slice(which * columns, (which + 1) * columns)
-        projected_ref[:, lanes] = (
-            total[which, 0:rows]
-            + full_in[which, 0].astype(F32)
-            + full_in[which, 1].astype(F32)
-            + bias_ref[:, lanes]
-        ).astype(BF16)
-        if which == 1:
-            keys = slice(2 * columns - behind.shape[1], 2 * columns)
-            net.start(
-                ("kv", 0), view(projected_ref, slice(None), keys), view(behind), 3, 1
-            )
+        sums_in(which, 1)
     net.finish()
     tables_ref[...] = tables[...]
     attend(projected_ref, behind, sinks_ref, attended, net.x * SIDE + net.z == 0)
@@ -762,11 +797,11 @@
         normed_ref[:, lanes] = (wide * inverse * mid_gain_ref[:, lanes]).astype(BF16)
 
 
-def attention_part(pieces, gains, state, weight, bias, ids, logits, sinks, out_weight, out_bias, mid_gain):
+def attention_part(state, gain, weight, bias, ids, logits, sinks, out_weight, out_bias, mid_gain):
     features, rows = state.shape
-    depth = pieces.shape[2]
+    depth = weight.shape[0]
     wide = weight.shape[1]
-    columns = wide // 2
+    columns = wide // 4
     keys = 2 * KEY_VALUE_HEADS * HEAD_DIM
     anywhere = pl.BlockSpec(memory_space=pl.ANY)
     vmem = pl.BlockSpec(memory_space=pltpu.VMEM)
@@ -778,7 +813,6 @@
             jax.ShapeDtypeStruct((SIDE, SIDE, 16, rows), F32),
         ),
         in_specs=[
-            vmem,
             vmem,
             vmem,
             anywhere,
@@ -793,21 +827,22 @@
         out_specs=(vmem, vmem, vmem),
         scratch_shapes=[
             pltpu.VMEM((rows, wide), BF16),
-            pltpu.VMEM(pieces.shape, BF16),
+            pltpu.VMEM((features, rows), F32),
+            pltpu.VMEM((SIDE, SIDE, depth, rows), BF16),
             pltpu.VMEM(out_weight.shape, BF16),
             pltpu.VMEM((QUERY_HEADS * HEAD_DIM, rows), BF16),
-            pltpu.VMEM((2, SIDE, depth, columns), BF16),
+            pltpu.VMEM((2, 2, SIDE, depth, columns), BF16),
             pltpu.VMEM((2, SIDE, depth, SIDE * rows), BF16),
             pltpu.VMEM((2, 2, 2, depth, rows), BF16),
-            pltpu.VMEM((2, SIDE * rows, columns), F32),
-            pltpu.VMEM((2, SIDE, rows, columns), BF16),
-            pltpu.VMEM((2, 2, rows, columns // 2), BF16),
-            pltpu.VMEM((2, 2, rows, columns), BF16),
+            pltpu.VMEM((2, 2, SIDE * rows, columns), F32),
+            pltpu.VMEM((2, 2, SIDE, rows, columns), BF16),
+            pltpu.VMEM((2, 2, 2, rows // 2, columns), BF16),
+            pltpu.VMEM((2, 2, 2, rows, columns), BF16),
             pltpu.VMEM((rows, keys), BF16),
             pltpu.VMEM((SIDE, SIDE, 16, rows), F32),
-            pltpu.SemaphoreType.DMA((5,)),
-            pltpu.SemaphoreType.DMA((48,)),
-            pltpu.SemaphoreType.DMA((48,)),
+            pltpu.SemaphoreType.DMA((9,)),
+            pltpu.SemaphoreType.DMA((64,)),
+            pltpu.SemaphoreType.DMA((64,)),
         ],
         compiler_params=pltpu.CompilerParams(
             collective_id=2, has_side_effects=True, vmem_limit_bytes=56 * 1024 * 1024
@@ -815,7 +850,7 @@
         cost_estimate=pl.CostEstimate(
             flops=2_000_000_000, bytes_accessed=4_000_000, transcendentals=0
         ),
-    )(pieces, gains, state, weight, bias, ids, logits, sinks, out_weight, out_bias, mid_gain)
+    )(state, gain, weight, bias, ids, logits, sinks, out_weight, out_bias, mid_gain)
 
 
 def shards(
@@ -833,16 +868,12 @@
     gate_logits,
     placement,
 ):
-    rows, features = section_input.shape[1:]
+    rows = section_input.shape[1]
     experts = placement.shape[1]
     slots = 2 * min(rows // 2, rows * TOP * 5 // (8 * experts))
-    depth = query_key_value_weight.shape[1]
-    state = section_input[0].T
-    apart = (SIDE, SIDE, depth, rows)
     normed_mid, residual, tables = attention_part(
-        state.reshape(apart),
-        jnp.broadcast_to(attention_gain[0].reshape(apart[:3])[..., None], apart),
-        state,
+        section_input[0].T,
+        attention_gain,
         query_key_value_weight[0],
         qkv_bias,
         expert_ids[0].T,

time: 209 us -> 199 us (0.952)
  Pallas kernels: 202 us -> 196 us
  local copies, waits for them, and re-layouts: 6.01 us -> 2.26 us
    pallas_call x1, Pallas kernels: 61.8 us -> 58.7 us  [attention_part(): pl.pallas_call(project_kernel, out_shape=(jax.ShapeDtypeStruct((rows, fea...]
    pallas_call x1, Pallas kernels: 140 us -> 137 us  [experts_and_pass(): pl.pallas_call(functools.partial(expert_kernel, slots), out_shape=jax.Sha...]
where the time goes in v5:
time: 199 us; the launch traced here: 198 us
  Pallas kernels  196 us (98%)
  local copies, waits for them, and re-layouts  2.26 us (1%)
    pallas_call x1, Pallas kernels, experts_and_pass(): pl.pallas_call(functools.partial(expert_kernel, slots), out_shape=jax.Sha...  137 us
    pallas_call x1, Pallas kernels, attention_part(): pl.pallas_call(project_kernel, out_shape=(jax.ShapeDtypeStruct((rows, fea...  58.7 us

profile of v5, /device:TPU:1, one launch (start us, length us, event | category | flops | bytes accessed | tf_op | source)
XLA Modules:
  0.0 198.4 jit_solution(5503795090543117973)
XLA Ops:
  0.0 58.7 %shard_map.127 = (bf16[128,2880]{1,0:T(8,128)(2,1)}, bf16[128,2880]{1,0:T(8,128)(2,1)}, f32[4,4,16,128]{3,2,1,0:T(8,128)}) custom-call(bf16[2880,128]{1,0:T(8,128)(2,1)} %bitcast.21, f32[1,2880]{1,0:T(1,128)} %gain_ref.1, bf16[180,2560]{1,0:T(8,128)(2,1)} %bitcast.19, f32[1,2560]{1,0:T(1,128)} %bias_ref.1, s32[4,128]{1,0:T(4,128)} %bitcast.22, ...), custom_call_target="tpu_custom_call" | custom-call | flops 2000000000 | bytes 4000000 | tf_op jit(solution)/shard_map/pallas_call | solution.py:808
  58.7 137.5 %shard_map.128 = bf16[128,2880]{1,0:T(8,128)(2,1)} custom-call(bf16[128,2880]{1,0:T(8,128)(2,1)} %get-tuple-element.8.normed_ref, bf16[128,2880]{1,0:T(8,128)(2,1)} %get-tuple-element.9.residual_ref, f32[4,4,16,128]{3,2,1,0:T(8,128)} %get-tuple-element.10.meta_ref, s32[1,8]{1,0:T(1,128)} %holders_ref.1, bf16[1440,2880]{1,0:T(8,128)(2,1)} %bitcast.24, ...), custom_call_target="tpu_custom_call" | custom-call | flops 16000000000 | bytes 16000000 | tf_op jit(solution)/shard_map/pallas_call | solution.py:445
  196.1 2.3 %copy.14 = bf16[1,128,2880]{1,2,0:T(8,128)(2,1)} copy(bf16[1,128,2880]{2,1,0:T(8,128)(2,1)} %bitcast.20) | data formatting | bytes 1474560 | tf_op jit(solution)/shard_map/broadcast_in_dim | solution.py:889

commit v6 on v5

--- a/solution.py
+++ b/solution.py
@@ -297,19 +297,22 @@
             relay(0)
         arrived(groups[at])
 
-    def relay(dp):
+    def relay(dp, pieces=1):
+        size = half_rows // pieces
         for which in (0, 1):
             for side, step in ((0, 1), (1, -1)):
                 net.need(("rh", which, dp, step))
                 there = part(which, dp, step % SIDE, at_of(step), quarter)
                 add_rows(there(), there(), half_in.at[which, dp, side])
-                net.start(
-                    ("rf", which, dp, step),
-                    part(which, dp, step % SIDE, 0, half_rows),
-                    view(full_in, which, dp, side),
-                    1 - which,
-                    step,
-                )
+                for piece in range(pieces):
+                    rows = slice(piece * size, (piece + 1) * size)
+                    net.start(
+                        ("rf", which, dp, step, piece),
+                        part(which, dp, step % SIDE, piece * size, size),
+                        view(full_in, which, dp, side, rows),
+                        1 - which,
+                        step,
+                    )
 
     def back(dp):
         for which in (0, 1):
@@ -372,11 +375,12 @@
     for dp in (2, 1, 3):
         back(dp)
 
-    def gather_in(dp):
-        for which in (0, 1):
-            net.need(("rf", which, dp, 1), ("rf", which, dp, -1))
-            here = part(which, dp, 0, 0, half_rows)
-            add_rows(here(), here(), full_in.at[which, dp, 0], full_in.at[which, dp, 1])
+    def gather_in(which, dp, piece=0, pieces=1):
+        size = half_rows // pieces
+        rows = slice(piece * size, (piece + 1) * size)
+        net.need(("rf", which, dp, 1, piece), ("rf", which, dp, -1, piece))
+        here = part(which, dp, 0, piece * size, size)
+        add_rows(here(), here(), full_in.at[which, dp, 0, rows], full_in.at[which, dp, 1, rows])
 
     def last_half(which):
         for side, step in ((0, 1), (1, -1)):
@@ -388,41 +392,46 @@
                 step,
             )
 
-    def last_full(step):
+    ends = ((0, quarter), (quarter, quarter // 2), (quarter * 3 // 2, quarter // 2))
+
+    def last_full(which, step, at, size):
         side = (1 - step) // 2
-        for which in (0, 1):
+        if at == at_of(step):
+            there = part(which, step % SIDE, 0, at, quarter)
             net.need(("lh", which, step))
-            there = part(which, step % SIDE, 0, at_of(step), quarter)
             add_rows(there(), there(), half_last.at[which, side])
-            for piece in (0, 1):
-                rows = slice(piece * quarter, (piece + 1) * quarter)
-                net.start(
-                    ("lf", which, step, piece),
-                    part(which, step % SIDE, 0, piece * quarter, quarter),
-                    view(full_last, which, side, rows),
-                    which,
-                    step,
-                )
+        net.start(
+            ("lf", which, step, at),
+            part(which, step % SIDE, 0, at, size),
+            view(full_last, which, side, slice(at, at + size)),
+            which,
+            step,
+        )
 
     relay(2)
     relay(1)
-    gather_in(2)
-    last_half(0)
-    last_half(1)
-    relay(3)
-    gather_in(1)
-    last_full(1)
-    gather_in(3)
-    last_full(-1)
     for which in (0, 1):
-        net.need(("rf", which, 0, 1), ("rf", which, 0, -1))
+        gather_in(which, 2)
+        last_half(which)
+    relay(3, 2)
+    for which in (0, 1):
+        gather_in(which, 1)
+        for at, size in ends:
+            last_full(which, 1, at, size)
     for piece in (0, 1):
         for which in (0, 1):
-            net.need(("lf", which, 1, piece), ("lf", which, -1, piece))
-            here = part(which, 0, 0, piece * quarter, quarter)
-            inside = slice(piece * quarter, (piece + 1) * quarter)
-            at = which * half_rows + piece * quarter
-            rows = slice(at, at + quarter)
+            gather_in(which, 3, piece, 2)
+            for at, size in ends:
+                if at // quarter == piece:
+                    last_full(which, -1, at, size)
+    for which in (0, 1):
+        net.need(("rf", which, 0, 1, 0), ("rf", which, 0, -1, 0))
+    for at, size in ends:
+        for which in (0, 1):
+            net.need(("lf", which, 1, at), ("lf", which, -1, at))
+            here = part(which, 0, 0, at, size)
+            inside = slice(at, at + size)
+            rows = slice(which * half_rows + at, which * half_rows + at + size)
             add_rows(
                 here(),
                 here(),
@@ -432,7 +441,7 @@
                 full_last.at[which, 1, inside],
                 residual_ref.at[rows],
             )
-            net.start(("out", which, piece), here, view(out_ref, rows), 2, 1)
+            net.start(("out", which, at), here, view(out_ref, rows), 2, 1)
     net.finish()
 
 
@@ -460,8 +469,8 @@
             pltpu.VMEM((2, 2, quarter, width), BF16),
             pltpu.VMEM((2, 2, half, width), BF16),
             pltpu.SemaphoreType.DMA((3,)),
-            pltpu.SemaphoreType.DMA((96,)),
-            pltpu.SemaphoreType.DMA((96,)),
+            pltpu.SemaphoreType.DMA((112,)),
+            pltpu.SemaphoreType.DMA((112,)),
         ],
         compiler_params=pltpu.CompilerParams(
             collective_id=1, has_side_effects=True, vmem_limit_bytes=62 * 1024 * 1024
@@ -484,7 +493,7 @@
     return member, weight
 
 
-def attend(projected, behind, sinks_ref, attended, first):
+def attend(groups, projected, behind, sinks_ref, attended, first):
     rows = projected.shape[0]
     pair = 2 * HEAD_DIM
     group = QUERY_HEADS // KEY_VALUE_HEADS
@@ -496,7 +505,7 @@
     offset = jnp.where(first, -1e30, 0.0)
     keys_at = QUERY_HEADS * HEAD_DIM
     values_at = keys_at + KEY_VALUE_HEADS * HEAD_DIM
-    for g in range(KEY_VALUE_HEADS):
+    for g in groups:
         tile = g // 2 * pair
         stacked = []
         own = projected[:, keys_at + tile : keys_at + tile + pair].astype(F32)
@@ -775,11 +784,14 @@
     for which in (1, 0):
         sums_on(which, 1)
     sums_in(0, 0)
+    first = net.x * SIDE + net.z == 0
+    net.need(("kv", 0))
+    attend((0,), projected_ref, behind, sinks_ref, attended, first)
     for which in (1, 0):
         sums_in(which, 1)
     net.finish()
     tables_ref[...] = tables[...]
-    attend(projected_ref, behind, sinks_ref, attended, net.x * SIDE + net.z == 0)
+    attend((1, 2, 3), projected_ref, behind, sinks_ref, attended, first)
     load_out.wait()
     squares = jnp.zeros((rows, 1), F32)
     for at, size in chunks(features, 640):

time: 199 us -> 197 us (0.990); the launches traced: 198 us -> 194 us
  Pallas kernels: 196 us -> 192 us
    pallas_call x1, Pallas kernels: 137 us -> 134 us  [experts_and_pass(): pl.pallas_call(functools.partial(expert_kernel, slots), out_shape=jax.Sha...]
where the time goes in v6:
time: 197 us; the launch traced here: 194 us
  Pallas kernels  192 us (97%)
  local copies, waits for them, and re-layouts  2.26 us (1%)
    pallas_call x1, Pallas kernels, experts_and_pass(): pl.pallas_call(functools.partial(expert_kernel, slots), out_shape=jax.Sha...  134 us
    pallas_call x1, Pallas kernels, attention_part(): pl.pallas_call(project_kernel, out_shape=(jax.ShapeDtypeStruct((rows, fea...  57.5 us

profile of v6, /device:TPU:1, one launch (start us, length us, event | category | flops | bytes accessed | tf_op | source)
XLA Modules:
  0.0 193.9 jit_solution(13680307918842933204)
XLA Ops:
  0.0 57.5 %shard_map.127 = (bf16[128,2880]{1,0:T(8,128)(2,1)}, bf16[128,2880]{1,0:T(8,128)(2,1)}, f32[4,4,16,128]{3,2,1,0:T(8,128)}) custom-call(bf16[2880,128]{1,0:T(8,128)(2,1)} %bitcast.21, f32[1,2880]{1,0:T(1,128)} %gain_ref.1, bf16[180,2560]{1,0:T(8,128)(2,1)} %bitcast.19, f32[1,2560]{1,0:T(1,128)} %bias_ref.1, s32[4,128]{1,0:T(4,128)} %bitcast.22, ...), custom_call_target="tpu_custom_call" | custom-call | flops 2000000000 | bytes 4000000 | tf_op jit(solution)/shard_map/pallas_call | solution.py:820
  57.5 134.1 %shard_map.128 = bf16[128,2880]{1,0:T(8,128)(2,1)} custom-call(bf16[128,2880]{1,0:T(8,128)(2,1)} %get-tuple-element.8.normed_ref, bf16[128,2880]{1,0:T(8,128)(2,1)} %get-tuple-element.9.residual_ref, f32[4,4,16,128]{3,2,1,0:T(8,128)} %get-tuple-element.10.meta_ref, s32[1,8]{1,0:T(1,128)} %holders_ref.1, bf16[1440,2880]{1,0:T(8,128)(2,1)} %bitcast.24, ...), custom_call_target="tpu_custom_call" | custom-call | flops 16000000000 | bytes 16000000 | tf_op jit(solution)/shard_map/pallas_call | solution.py:454
  191.6 2.3 %copy.14 = bf16[1,128,2880]{1,2,0:T(8,128)(2,1)} copy(bf16[1,128,2880]{2,1,0:T(8,128)(2,1)} %bitcast.20) | data formatting | bytes 1474560 | tf_op jit(solution)/shard_map/broadcast_in_dim | solution.py:901

commit v7 on v6

--- a/solution.py
+++ b/solution.py
@@ -493,7 +493,7 @@
     return member, weight
 
 
-def attend(groups, projected, behind, sinks_ref, attended, first):
+def attend(pairs, projected, behind, sinks_ref, attended, first):
     rows = projected.shape[0]
     pair = 2 * HEAD_DIM
     group = QUERY_HEADS // KEY_VALUE_HEADS
@@ -505,7 +505,7 @@
     offset = jnp.where(first, -1e30, 0.0)
     keys_at = QUERY_HEADS * HEAD_DIM
     values_at = keys_at + KEY_VALUE_HEADS * HEAD_DIM
-    for g in groups:
+    for g in sorted({head // group for head in pairs}):
         tile = g // 2 * pair
         stacked = []
         own = projected[:, keys_at + tile : keys_at + tile + pair].astype(F32)
@@ -524,7 +524,7 @@
             axis=0,
         ).astype(F32)
         values = values.T[g % 2 * HEAD_DIM : (g % 2 + 1) * HEAD_DIM].astype(BF16)
-        for head in range(g * group, (g + 1) * group, 2):
+        for head in [head for head in pairs if head // group == g]:
             scores = across(keys, projected[:, head * HEAD_DIM : head * HEAD_DIM + pair])
             for side in (0, 1):
                 past = scores[2 * side * rows : (2 * side + 1) * rows]
@@ -786,18 +786,27 @@
     sums_in(0, 0)
     first = net.x * SIDE + net.z == 0
     net.need(("kv", 0))
-    attend((0,), projected_ref, behind, sinks_ref, attended, first)
+    early = (0, 2, 4, 6, 8, 30)
+    attend(early, projected_ref, behind, sinks_ref, attended, first)
+    known = 8 * HEAD_DIM
+    load_out.wait()
+    for at, size in chunks(features, 640):
+        lanes = slice(at, at + size)
+        scaled[lanes] = state_ref[lanes].astype(F32) + jnp.dot(
+            out_weight[lanes, :known], attended[:known], preferred_element_type=F32
+        )
     for which in (1, 0):
         sums_in(which, 1)
     net.finish()
     tables_ref[...] = tables[...]
-    attend((1, 2, 3), projected_ref, behind, sinks_ref, attended, first)
-    load_out.wait()
+    late = [head for head in range(0, QUERY_HEADS, 2) if head not in early]
+    attend(late, projected_ref, behind, sinks_ref, attended, first)
     squares = jnp.zeros((rows, 1), F32)
     for at, size in chunks(features, 640):
         lanes = slice(at, at + size)
-        mixed = jnp.dot(out_weight[lanes], attended[...], preferred_element_type=F32)
-        mixed = mixed + state_ref[lanes].astype(F32)
+        mixed = scaled[lanes] + jnp.dot(
+            out_weight[lanes, known:], attended[known:], preferred_element_type=F32
+        )
         kept_sum = (mixed.T + out_bias_ref[:, lanes]).astype(BF16)
         residual_ref[:, lanes] = kept_sum
         wide = kept_sum.astype(F32)

time: 197 us -> 195 us (0.990); the launches traced: 194 us -> 195 us
    pallas_call x1, Pallas kernels: 134 us -> 136 us  [experts_and_pass(): pl.pallas_call(functools.partial(expert_kernel, slots), out_shape=jax.Sha...]
where the time goes in v7:
time: 195 us
  Pallas kernels  192 us (98%)
  local copies, waits for them, and re-layouts  2.26 us (1%)
    pallas_call x1, Pallas kernels, experts_and_pass(): pl.pallas_call(functools.partial(expert_kernel, slots), out_shape=jax.Sha...  136 us
    pallas_call x1, Pallas kernels, attention_part(): pl.pallas_call(project_kernel, out_shape=(jax.ShapeDtypeStruct((rows, fea...  56 us

profile of v7, /device:TPU:1, one launch (start us, length us, event | category | flops | bytes accessed | tf_op | source)
XLA Modules:
  0.0 194.7 jit_solution(6494484152642549779)
XLA Ops:
  0.0 56.0 %shard_map.127 = (bf16[128,2880]{1,0:T(8,128)(2,1)}, bf16[128,2880]{1,0:T(8,128)(2,1)}, f32[4,4,16,128]{3,2,1,0:T(8,128)}) custom-call(bf16[2880,128]{1,0:T(8,128)(2,1)} %bitcast.21, f32[1,2880]{1,0:T(1,128)} %gain_ref.1, bf16[180,2560]{1,0:T(8,128)(2,1)} %bitcast.19, f32[1,2560]{1,0:T(1,128)} %bias_ref.1, s32[4,128]{1,0:T(4,128)} %bitcast.22, ...), custom_call_target="tpu_custom_call" | custom-call | flops 2000000000 | bytes 4000000 | tf_op jit(solution)/shard_map/pallas_call | solution.py:829
  56.0 136.5 %shard_map.128 = bf16[128,2880]{1,0:T(8,128)(2,1)} custom-call(bf16[128,2880]{1,0:T(8,128)(2,1)} %get-tuple-element.8.normed_ref, bf16[128,2880]{1,0:T(8,128)(2,1)} %get-tuple-element.9.residual_ref, f32[4,4,16,128]{3,2,1,0:T(8,128)} %get-tuple-element.10.meta_ref, s32[1,8]{1,0:T(1,128)} %holders_ref.1, bf16[1440,2880]{1,0:T(8,128)(2,1)} %bitcast.24, ...), custom_call_target="tpu_custom_call" | custom-call | flops 16000000000 | bytes 16000000 | tf_op jit(solution)/shard_map/pallas_call | solution.py:454
  192.5 2.3 %copy.14 = bf16[1,128,2880]{1,2,0:T(8,128)(2,1)} copy(bf16[1,128,2880]{2,1,0:T(8,128)(2,1)} %bitcast.20) | data formatting | bytes 1474560 | tf_op jit(solution)/shard_map/broadcast_in_dim | solution.py:910
